TPU v7x, 768 devices: a whole 4x8x12 slice. The times are simulated.
768 devices in a mesh: dp: 12 (over z_lo, x), seq: 32 (over y, z_hi), head: 2 (over core).
Axes of the slice: x: 4, y: 8, z: 12 (z_hi: 4, z_lo: 3; z = z_hi * 3 + z_lo), core: 2. Of those that a mesh axis runs over, the one named last changes fastest.
Arguments:
- q_img: bfloat16 [12, 5632, 1536], P('dp', 'seq', 'head'), may hold values from -51 to 51
- k_img: bfloat16 [12, 5632, 1536], P('dp', 'seq', 'head'), may hold values from -4 to 4
- v_img: bfloat16 [12, 5632, 1536], P('dp', 'seq', 'head'), may hold values from -6 to 6
- k_txt: bfloat16 [12, 512, 1536], P('dp', 'seq', 'head'), may hold values from -6 to 6
- v_txt: bfloat16 [12, 512, 1536], P('dp', 'seq', 'head'), may hold values from -6 to 6
- text_length: int32 [12, 2], P('dp'), may hold values from 1 to 256, as said below
- w_out: bfloat16 [1536, 3072], P('head'), may hold values from -4 to 4
- branch_gate: float32 [3072], P('dp'), may hold values from 0.5 to 2
Outputs:
- branch_out: bfloat16 [12, 5632, 3072], P('dp', 'seq', 'head')
Inputs may be any that keep to these rules, and one draw needn't show every extreme that they name: `text_length`: some sample has all 256 text slots live.
All inputs are finite; a program needn't handle non-finite values.
Results may differ from a plain program's by a relative error of at most 0.014.
Values may be sent and summed in bfloat16 or wider, within the bound.
No kernel may reach another device: no remote copies, remote signals or barrier semaphores. Data moves between devices by JAX's collectives and lax.ppermute only.
A program may use at most 32 MiB of HBM per device.

v0:
```python
import math

import jax
import jax.numpy as jnp
from jax import lax
from jax.sharding import PartitionSpec as P

HEAD_DIM = 128


def shifted(array, axis, by):
    length = lax.axis_size(axis)
    return lax.ppermute(array, axis, [(i, (i + by) % length) for i in range(length)])


def absorb(carried, queries, key_block, value_block, usable):
    maxima, totals, accumulated = carried
    head_count = queries.shape[1]
    key_heads = key_block.reshape(key_block.shape[0], head_count, HEAD_DIM)
    value_heads = value_block.reshape(value_block.shape[0], head_count, HEAD_DIM)
    scores = jnp.einsum("qhd,khd->hqk", queries, key_heads, preferred_element_type=jnp.float32) * (
        1.0 / math.sqrt(HEAD_DIM)
    )
    scores = jnp.where(usable[None, None, :], scores, -jnp.inf)
    new_max = jnp.maximum(maxima, jnp.max(scores, axis=2))
    rescale = jnp.exp(maxima - new_max)
    weights = jnp.exp(scores - new_max[:, :, None])
    totals = totals * rescale + jnp.sum(weights, axis=2)
    accumulated = accumulated * rescale[:, :, None] + jnp.einsum(
        "hqk,khd->hqd",
        weights.astype(jnp.bfloat16),
        value_heads,
        preferred_element_type=jnp.float32,
    )
    return (new_max, totals, accumulated)


def per_device(q_img, k_img, v_img, k_txt, v_txt, text_length, w_out, branch_gate):
    row_count = q_img.shape[1]
    head_count = q_img.shape[2] // HEAD_DIM
    queries = q_img[0].reshape(row_count, head_count, HEAD_DIM)
    seq_count = lax.axis_size("seq")
    half_count = seq_count // 2
    position = lax.axis_index("seq")
    parity = position % 2
    live_text = lax.dynamic_index_in_dim(text_length[0], parity, 0, keepdims=False)
    image_slots = k_img.shape[1]
    text_slots = k_txt.shape[1]
    half_slots = text_slots // 2
    feature_width = k_txt.shape[2]
    start_state = (
        jnp.full((head_count, row_count), -1e30, jnp.float32),
        jnp.zeros((head_count, row_count), jnp.float32),
        jnp.zeros((head_count, row_count, HEAD_DIM), jnp.float32),
    )
    text_both = jnp.stack([k_txt[0], v_txt[0]])
    text_all = lax.all_gather(text_both, "seq", axis=1, tiled=True)
    text_all = text_all.reshape(2, seq_count, 2, half_slots, feature_width)
    text_own = lax.dynamic_index_in_dim(text_all, parity, 2, keepdims=False).reshape(
        2, seq_count * half_slots, feature_width
    )
    text_usable = jnp.arange(seq_count * half_slots, dtype=jnp.int32) < live_text
    state_after = absorb(start_state, queries, text_own[0], text_own[1], text_usable)
    image_pair = jnp.stack([k_img[0], v_img[0]])
    image_usable = jnp.ones((image_slots,), dtype=bool)
    first_state = absorb(state_after, queries, image_pair[0], image_pair[1], image_usable)

    def image_turn(turn, carry):
        state, block = carry
        block = shifted(block, "seq", 2)
        return (absorb(state, queries, block[0], block[1], image_usable), block)

    final_state, unused = lax.fori_loop(0, half_count - 1, image_turn, (first_state, image_pair))
    maxima, totals, accumulated = final_state
    attended = (
        (accumulated / totals[:, :, None])
        .transpose(1, 0, 2)
        .reshape(row_count, head_count * HEAD_DIM)
        .astype(jnp.bfloat16)
    )
    projected = jnp.dot(attended, w_out, preferred_element_type=jnp.float32)
    column_share = lax.psum_scatter(
        projected[None].astype(jnp.bfloat16), "head", scatter_dimension=2, tiled=True
    ).astype(jnp.float32)
    gate_whole = lax.all_gather(branch_gate, "dp", axis=0, tiled=True)
    share_width = column_share.shape[2]
    gate_part = lax.dynamic_slice_in_dim(
        gate_whole, lax.axis_index("head") * share_width, share_width
    )
    return (column_share * gate_part).astype(jnp.bfloat16)


def solution(mesh):
    in_specs = (
        P("dp", "seq", "head"),
        P("dp", "seq", "head"),
        P("dp", "seq", "head"),
        P("dp", "seq", "head"),
        P("dp", "seq", "head"),
        P("dp", None),
        P("head", None),
        P("dp"),
    )
    out_specs = P("dp", "seq", "head")
    return jax.shard_map(
        per_device, mesh=mesh, in_specs=in_specs, out_specs=out_specs, check_vma=False
    )
```

profile of v0, /device:TPU:138, one launch (start us, length us, event | category | flops | bytes accessed | tf_op | source)
XLA Modules:
  0.0 815.0 jit_solution(8993259974250045275)
XLA Ops:
  6.5 1.4 pad_maximum_fusion.1
  8.1 1.3 reshape_squeeze.10
  9.7 1.1 reshape_squeeze_stack_squeeze.7
  10.8 0.6 constant_dynamic-slice_fusion
  11.4 0.6 iota_compare_fusion
  12.1 0.8 pad_maximum_fusion
  13.3 97.7 %all-gather.3.cloned.1.call-done = bf16[2,512,768]{2,1,0:T(8,128)(2,1)} async-done(((bf16[2,16,768]{2,1,0:T(8,128)(2,1)}), bf16[2,512,768]{2,1,0:T(8,128)(2,1)}) %all-gather.3.cloned.1.call-update) | async-done | bytes 1572880 | tf_op jit(solution)/shard_map/all_gather | solution.py:57
  111.0 1.2 dynamic-slice_bitcast_fusion
  113.6 1.2 fusion.15
  116.9 569.7 %while.16 = (s32[]{:T(128)}, f32[6,176]{1,0:T(8,128)S(1)}, f32[6,176]{1,0:T(8,128)S(1)}, f32[6,176,128]{2,1,0:T(8,128)S(1)}, bf16[2,176,768]{2,1,0:T(8,128)(2,1)...) while((s32[]{:T(128)}, f32[6,176]{1,0:T(8,128)S(1)}, f32[6,176]{1,0:T(8,128)S(1)}, ...), condition=%wide.region_7.8_spmd, body=%wide.region_4.7_spmd.sunk | while | flops 96545856 | bytes 9597045 | solution.py:73
  116.9 3.6 collective-permute-start
  120.4 39.8 %collective-permute-done = bf16[2,176,768]{2,1,0:T(8,128)(2,1)S(1)} collective-permute-done((bf16[2,176,768]{2,1,0:T(8,128)(2,1)S(1)}, bf16[2,176,768]{2,1,0:T(8,128)(2,1)S(1)}, u32[]{:S(2)}, u32[]{:S(2)}) %collective-permute-start) | collective-permute-done | bytes 540704 | tf_op jit(solution)/shard_map/while/body/eval_jaxpr/ppermute | solution.py:13
  162.2 1.9 collective-permute-start
  164.2 25.8 %collective-permute-done = bf16[2,176,768]{2,1,0:T(8,128)(2,1)S(1)} collective-permute-done((bf16[2,176,768]{2,1,0:T(8,128)(2,1)S(1)}, bf16[2,176,768]{2,1,0:T(8,128)(2,1)S(1)}, u32[]{:S(2)}, u32[]{:S(2)}) %collective-permute-start) | collective-permute-done | bytes 540704 | tf_op jit(solution)/shard_map/while/body/eval_jaxpr/ppermute | solution.py:13
  192.0 2.8 collective-permute-start
  194.7 29.5 %collective-permute-done = bf16[2,176,768]{2,1,0:T(8,128)(2,1)S(1)} collective-permute-done((bf16[2,176,768]{2,1,0:T(8,128)(2,1)S(1)}, bf16[2,176,768]{2,1,0:T(8,128)(2,1)S(1)}, u32[]{:S(2)}, u32[]{:S(2)}) %collective-permute-start) | collective-permute-done | bytes 540704 | tf_op jit(solution)/shard_map/while/body/eval_jaxpr/ppermute | solution.py:13
  226.2 4.5 collective-permute-start
  230.7 34.2 %collective-permute-done = bf16[2,176,768]{2,1,0:T(8,128)(2,1)S(1)} collective-permute-done((bf16[2,176,768]{2,1,0:T(8,128)(2,1)S(1)}, bf16[2,176,768]{2,1,0:T(8,128)(2,1)S(1)}, u32[]{:S(2)}, u32[]{:S(2)}) %collective-permute-start) | collective-permute-done | bytes 540704 | tf_op jit(solution)/shard_map/while/body/eval_jaxpr/ppermute | solution.py:13
  266.8 4.7 collective-permute-start
  271.5 29.5 %collective-permute-done = bf16[2,176,768]{2,1,0:T(8,128)(2,1)S(1)} collective-permute-done((bf16[2,176,768]{2,1,0:T(8,128)(2,1)S(1)}, bf16[2,176,768]{2,1,0:T(8,128)(2,1)S(1)}, u32[]{:S(2)}, u32[]{:S(2)}) %collective-permute-start) | collective-permute-done | bytes 540704 | tf_op jit(solution)/shard_map/while/body/eval_jaxpr/ppermute | solution.py:13
  302.2 0.6 convolution_add_fusion.3
  302.9 4.5 collective-permute-start
  307.4 34.2 %collective-permute-done = bf16[2,176,768]{2,1,0:T(8,128)(2,1)S(1)} collective-permute-done((bf16[2,176,768]{2,1,0:T(8,128)(2,1)S(1)}, bf16[2,176,768]{2,1,0:T(8,128)(2,1)S(1)}, u32[]{:S(2)}, u32[]{:S(2)}) %collective-permute-start) | collective-permute-done | bytes 540704 | tf_op jit(solution)/shard_map/while/body/eval_jaxpr/ppermute | solution.py:13
  342.8 0.6 convolution_add_fusion.3
  343.5 4.7 collective-permute-start
  348.2 29.5 %collective-permute-done = bf16[2,176,768]{2,1,0:T(8,128)(2,1)S(1)} collective-permute-done((bf16[2,176,768]{2,1,0:T(8,128)(2,1)S(1)}, bf16[2,176,768]{2,1,0:T(8,128)(2,1)S(1)}, u32[]{:S(2)}, u32[]{:S(2)}) %collective-permute-start) | collective-permute-done | bytes 540704 | tf_op jit(solution)/shard_map/while/body/eval_jaxpr/ppermute | solution.py:13
  379.7 4.5 collective-permute-start
  384.1 34.2 %collective-permute-done = bf16[2,176,768]{2,1,0:T(8,128)(2,1)S(1)} collective-permute-done((bf16[2,176,768]{2,1,0:T(8,128)(2,1)S(1)}, bf16[2,176,768]{2,1,0:T(8,128)(2,1)S(1)}, u32[]{:S(2)}, u32[]{:S(2)}) %collective-permute-start) | collective-permute-done | bytes 540704 | tf_op jit(solution)/shard_map/while/body/eval_jaxpr/ppermute | solution.py:13
  420.2 4.7 collective-permute-start
  424.9 29.5 %collective-permute-done = bf16[2,176,768]{2,1,0:T(8,128)(2,1)S(1)} collective-permute-done((bf16[2,176,768]{2,1,0:T(8,128)(2,1)S(1)}, bf16[2,176,768]{2,1,0:T(8,128)(2,1)S(1)}, u32[]{:S(2)}, u32[]{:S(2)}) %collective-permute-start) | collective-permute-done | bytes 540704 | tf_op jit(solution)/shard_map/while/body/eval_jaxpr/ppermute | solution.py:13
  455.7 0.6 convolution_add_fusion.3
  456.4 4.5 collective-permute-start
  460.9 34.2 %collective-permute-done = bf16[2,176,768]{2,1,0:T(8,128)(2,1)S(1)} collective-permute-done((bf16[2,176,768]{2,1,0:T(8,128)(2,1)S(1)}, bf16[2,176,768]{2,1,0:T(8,128)(2,1)S(1)}, u32[]{:S(2)}, u32[]{:S(2)}) %collective-permute-start) | collective-permute-done | bytes 540704 | tf_op jit(solution)/shard_map/while/body/eval_jaxpr/ppermute | solution.py:13
  496.3 0.6 convolution_add_fusion.3
  497.0 4.7 collective-permute-start
  501.6 29.5 %collective-permute-done = bf16[2,176,768]{2,1,0:T(8,128)(2,1)S(1)} collective-permute-done((bf16[2,176,768]{2,1,0:T(8,128)(2,1)S(1)}, bf16[2,176,768]{2,1,0:T(8,128)(2,1)S(1)}, u32[]{:S(2)}, u32[]{:S(2)}) %collective-permute-start) | collective-permute-done | bytes 540704 | tf_op jit(solution)/shard_map/while/body/eval_jaxpr/ppermute | solution.py:13
  533.1 4.5 collective-permute-start
  537.6 34.2 %collective-permute-done = bf16[2,176,768]{2,1,0:T(8,128)(2,1)S(1)} collective-permute-done((bf16[2,176,768]{2,1,0:T(8,128)(2,1)S(1)}, bf16[2,176,768]{2,1,0:T(8,128)(2,1)S(1)}, u32[]{:S(2)}, u32[]{:S(2)}) %collective-permute-start) | collective-permute-done | bytes 540704 | tf_op jit(solution)/shard_map/while/body/eval_jaxpr/ppermute | solution.py:13
  573.7 4.7 collective-permute-start
  578.4 29.5 %collective-permute-done = bf16[2,176,768]{2,1,0:T(8,128)(2,1)S(1)} collective-permute-done((bf16[2,176,768]{2,1,0:T(8,128)(2,1)S(1)}, bf16[2,176,768]{2,1,0:T(8,128)(2,1)S(1)}, u32[]{:S(2)}, u32[]{:S(2)}) %collective-permute-start) | collective-permute-done | bytes 540704 | tf_op jit(solution)/shard_map/while/body/eval_jaxpr/ppermute | solution.py:13
  609.9 4.5 collective-permute-start
  614.3 34.2 %collective-permute-done = bf16[2,176,768]{2,1,0:T(8,128)(2,1)S(1)} collective-permute-done((bf16[2,176,768]{2,1,0:T(8,128)(2,1)S(1)}, bf16[2,176,768]{2,1,0:T(8,128)(2,1)S(1)}, u32[]{:S(2)}, u32[]{:S(2)}) %collective-permute-start) | collective-permute-done | bytes 540704 | tf_op jit(solution)/shard_map/while/body/eval_jaxpr/ppermute | solution.py:13
  650.4 4.7 collective-permute-start
  655.1 29.5 %collective-permute-done = bf16[2,176,768]{2,1,0:T(8,128)(2,1)S(1)} collective-permute-done((bf16[2,176,768]{2,1,0:T(8,128)(2,1)S(1)}, bf16[2,176,768]{2,1,0:T(8,128)(2,1)S(1)}, u32[]{:S(2)}, u32[]{:S(2)}) %collective-permute-start) | collective-permute-done | bytes 540704 | tf_op jit(solution)/shard_map/while/body/eval_jaxpr/ppermute | solution.py:13
  686.5 4.4 fusion.6
  691.0 0.6 copy-done.6
  691.6 114.5 %all-gather = f32[12,1,256]{2,1,0:T(1,128)S(1)} all-gather(f32[1,1,256]{2,1,0:T(1,128)S(1)} %bitcast.37), channel_id=1, replica_groups=mesh['dp'=12,'seq'=32,'head'=2] {'dp'}, dimensions={0}, use_global_device_ids=true | all-gather | bytes 13312 | tf_op jit(solution)/shard_map/all_gather | solution.py:85
  806.2 1.9 multiply_convert_fusion
  (176 shorter events, 29.7 us)
Async XLA Ops:
  6.5 4.3 copy-start
  6.5 2.9 copy-start.3
  6.5 3.2 copy-start.4
  6.5 104.4 %all-gather.3.cloned.1.call-start = ((), (), s32[]{:S(2)}) async-start(), calls=%async_computation.1 | async-start | bytes 1622016 | tf_op jit(solution)/shard_map/all_gather | solution.py:57
  8.0 798.2 %reduce-scatter.2.cloned.1.call-start = ((), (), s32[]{:S(2)}) async-start(), calls=%async_computation.2 | async-start | bytes 1622016 | tf_op jit(solution)/shard_map/reduce_scatter | solution.py:82
  112.6 1.0 copy-start.2
  114.8 1.0 copy-start.1
  115.8 1.0 copy-start.5
  116.9 43.4 %collective-permute-start = (bf16[2,176,768]{2,1,0:T(8,128)(2,1)S(1)}, bf16[2,176,768]{2,1,0:T(8,128)(2,1)S(1)}, u32[]{:S(2)}, u32[]{:S(2)}) collective-permute-start(bf16[2,176,768]{2,1,0:T(8,128)(2,1)S(1)} %get-tuple-element.141), channel_id=1, source_target_pairs={{0,4},{2,6},{4,8},{6,10},{8,12},{10,14},{12,16},{14,18},{16,20},{1... | collective-permute-start | bytes 1622024 | tf_op jit(solution)/shard_map/while/body/eval_jaxpr/ppermute | solution.py:13
  162.2 27.8 %collective-permute-start = (bf16[2,176,768]{2,1,0:T(8,128)(2,1)S(1)}, bf16[2,176,768]{2,1,0:T(8,128)(2,1)S(1)}, u32[]{:S(2)}, u32[]{:S(2)}) collective-permute-start(bf16[2,176,768]{2,1,0:T(8,128)(2,1)S(1)} %get-tuple-element.141), channel_id=1, source_target_pairs={{0,4},{2,6},{4,8},{6,10},{8,12},{10,14},{12,16},{14,18},{16,20},{1... | collective-permute-start | bytes 1622024 | tf_op jit(solution)/shard_map/while/body/eval_jaxpr/ppermute | solution.py:13
  192.0 32.3 %collective-permute-start = (bf16[2,176,768]{2,1,0:T(8,128)(2,1)S(1)}, bf16[2,176,768]{2,1,0:T(8,128)(2,1)S(1)}, u32[]{:S(2)}, u32[]{:S(2)}) collective-permute-start(bf16[2,176,768]{2,1,0:T(8,128)(2,1)S(1)} %get-tuple-element.141), channel_id=1, source_target_pairs={{0,4},{2,6},{4,8},{6,10},{8,12},{10,14},{12,16},{14,18},{16,20},{1... | collective-permute-start | bytes 1622024 | tf_op jit(solution)/shard_map/while/body/eval_jaxpr/ppermute | solution.py:13
  226.2 38.6 %collective-permute-start = (bf16[2,176,768]{2,1,0:T(8,128)(2,1)S(1)}, bf16[2,176,768]{2,1,0:T(8,128)(2,1)S(1)}, u32[]{:S(2)}, u32[]{:S(2)}) collective-permute-start(bf16[2,176,768]{2,1,0:T(8,128)(2,1)S(1)} %get-tuple-element.141), channel_id=1, source_target_pairs={{0,4},{2,6},{4,8},{6,10},{8,12},{10,14},{12,16},{14,18},{16,20},{1... | collective-permute-start | bytes 1622024 | tf_op jit(solution)/shard_map/while/body/eval_jaxpr/ppermute | solution.py:13
  266.8 34.2 %collective-permute-start = (bf16[2,176,768]{2,1,0:T(8,128)(2,1)S(1)}, bf16[2,176,768]{2,1,0:T(8,128)(2,1)S(1)}, u32[]{:S(2)}, u32[]{:S(2)}) collective-permute-start(bf16[2,176,768]{2,1,0:T(8,128)(2,1)S(1)} %get-tuple-element.141), channel_id=1, source_target_pairs={{0,4},{2,6},{4,8},{6,10},{8,12},{10,14},{12,16},{14,18},{16,20},{1... | collective-permute-start | bytes 1622024 | tf_op jit(solution)/shard_map/while/body/eval_jaxpr/ppermute | solution.py:13
  302.9 38.6 %collective-permute-start = (bf16[2,176,768]{2,1,0:T(8,128)(2,1)S(1)}, bf16[2,176,768]{2,1,0:T(8,128)(2,1)S(1)}, u32[]{:S(2)}, u32[]{:S(2)}) collective-permute-start(bf16[2,176,768]{2,1,0:T(8,128)(2,1)S(1)} %get-tuple-element.141), channel_id=1, source_target_pairs={{0,4},{2,6},{4,8},{6,10},{8,12},{10,14},{12,16},{14,18},{16,20},{1... | collective-permute-start | bytes 1622024 | tf_op jit(solution)/shard_map/while/body/eval_jaxpr/ppermute | solution.py:13
  343.5 34.2 %collective-permute-start = (bf16[2,176,768]{2,1,0:T(8,128)(2,1)S(1)}, bf16[2,176,768]{2,1,0:T(8,128)(2,1)S(1)}, u32[]{:S(2)}, u32[]{:S(2)}) collective-permute-start(bf16[2,176,768]{2,1,0:T(8,128)(2,1)S(1)} %get-tuple-element.141), channel_id=1, source_target_pairs={{0,4},{2,6},{4,8},{6,10},{8,12},{10,14},{12,16},{14,18},{16,20},{1... | collective-permute-start | bytes 1622024 | tf_op jit(solution)/shard_map/while/body/eval_jaxpr/ppermute | solution.py:13
  379.7 38.6 %collective-permute-start = (bf16[2,176,768]{2,1,0:T(8,128)(2,1)S(1)}, bf16[2,176,768]{2,1,0:T(8,128)(2,1)S(1)}, u32[]{:S(2)}, u32[]{:S(2)}) collective-permute-start(bf16[2,176,768]{2,1,0:T(8,128)(2,1)S(1)} %get-tuple-element.141), channel_id=1, source_target_pairs={{0,4},{2,6},{4,8},{6,10},{8,12},{10,14},{12,16},{14,18},{16,20},{1... | collective-permute-start | bytes 1622024 | tf_op jit(solution)/shard_map/while/body/eval_jaxpr/ppermute | solution.py:13
  420.2 34.2 %collective-permute-start = (bf16[2,176,768]{2,1,0:T(8,128)(2,1)S(1)}, bf16[2,176,768]{2,1,0:T(8,128)(2,1)S(1)}, u32[]{:S(2)}, u32[]{:S(2)}) collective-permute-start(bf16[2,176,768]{2,1,0:T(8,128)(2,1)S(1)} %get-tuple-element.141), channel_id=1, source_target_pairs={{0,4},{2,6},{4,8},{6,10},{8,12},{10,14},{12,16},{14,18},{16,20},{1... | collective-permute-start | bytes 1622024 | tf_op jit(solution)/shard_map/while/body/eval_jaxpr/ppermute | solution.py:13
  456.4 38.6 %collective-permute-start = (bf16[2,176,768]{2,1,0:T(8,128)(2,1)S(1)}, bf16[2,176,768]{2,1,0:T(8,128)(2,1)S(1)}, u32[]{:S(2)}, u32[]{:S(2)}) collective-permute-start(bf16[2,176,768]{2,1,0:T(8,128)(2,1)S(1)} %get-tuple-element.141), channel_id=1, source_target_pairs={{0,4},{2,6},{4,8},{6,10},{8,12},{10,14},{12,16},{14,18},{16,20},{1... | collective-permute-start | bytes 1622024 | tf_op jit(solution)/shard_map/while/body/eval_jaxpr/ppermute | solution.py:13
  497.0 34.2 %collective-permute-start = (bf16[2,176,768]{2,1,0:T(8,128)(2,1)S(1)}, bf16[2,176,768]{2,1,0:T(8,128)(2,1)S(1)}, u32[]{:S(2)}, u32[]{:S(2)}) collective-permute-start(bf16[2,176,768]{2,1,0:T(8,128)(2,1)S(1)} %get-tuple-element.141), channel_id=1, source_target_pairs={{0,4},{2,6},{4,8},{6,10},{8,12},{10,14},{12,16},{14,18},{16,20},{1... | collective-permute-start | bytes 1622024 | tf_op jit(solution)/shard_map/while/body/eval_jaxpr/ppermute | solution.py:13
  533.1 38.6 %collective-permute-start = (bf16[2,176,768]{2,1,0:T(8,128)(2,1)S(1)}, bf16[2,176,768]{2,1,0:T(8,128)(2,1)S(1)}, u32[]{:S(2)}, u32[]{:S(2)}) collective-permute-start(bf16[2,176,768]{2,1,0:T(8,128)(2,1)S(1)} %get-tuple-element.141), channel_id=1, source_target_pairs={{0,4},{2,6},{4,8},{6,10},{8,12},{10,14},{12,16},{14,18},{16,20},{1... | collective-permute-start | bytes 1622024 | tf_op jit(solution)/shard_map/while/body/eval_jaxpr/ppermute | solution.py:13
  573.7 34.2 %collective-permute-start = (bf16[2,176,768]{2,1,0:T(8,128)(2,1)S(1)}, bf16[2,176,768]{2,1,0:T(8,128)(2,1)S(1)}, u32[]{:S(2)}, u32[]{:S(2)}) collective-permute-start(bf16[2,176,768]{2,1,0:T(8,128)(2,1)S(1)} %get-tuple-element.141), channel_id=1, source_target_pairs={{0,4},{2,6},{4,8},{6,10},{8,12},{10,14},{12,16},{14,18},{16,20},{1... | collective-permute-start | bytes 1622024 | tf_op jit(solution)/shard_map/while/body/eval_jaxpr/ppermute | solution.py:13
  609.9 38.6 %collective-permute-start = (bf16[2,176,768]{2,1,0:T(8,128)(2,1)S(1)}, bf16[2,176,768]{2,1,0:T(8,128)(2,1)S(1)}, u32[]{:S(2)}, u32[]{:S(2)}) collective-permute-start(bf16[2,176,768]{2,1,0:T(8,128)(2,1)S(1)} %get-tuple-element.141), channel_id=1, source_target_pairs={{0,4},{2,6},{4,8},{6,10},{8,12},{10,14},{12,16},{14,18},{16,20},{1... | collective-permute-start | bytes 1622024 | tf_op jit(solution)/shard_map/while/body/eval_jaxpr/ppermute | solution.py:13
  650.4 34.2 %collective-permute-start = (bf16[2,176,768]{2,1,0:T(8,128)(2,1)S(1)}, bf16[2,176,768]{2,1,0:T(8,128)(2,1)S(1)}, u32[]{:S(2)}, u32[]{:S(2)}) collective-permute-start(bf16[2,176,768]{2,1,0:T(8,128)(2,1)S(1)} %get-tuple-element.141), channel_id=1, source_target_pairs={{0,4},{2,6},{4,8},{6,10},{8,12},{10,14},{12,16},{14,18},{16,20},{1... | collective-permute-start | bytes 1622024 | tf_op jit(solution)/shard_map/while/body/eval_jaxpr/ppermute | solution.py:13
  690.9 0.7 copy-start.6
Sparse Core Ops, SparseCore 0:
  11.0 99.8 all-gather.2
  691.1 101.8 reduce-scatter.1
where the time goes:
time: 816 us; the launch traced here: 815 us
  waiting for transfers between devices  575 us (70%)
  blocking collectives  115 us (14%)
  starting transfers between devices  63.1 us (8%)
  matrix products  21.4 us (3%)
  local copies, waits for them, and re-layouts  17.7 us (2%)
  between operations  13.5 us (2%)
  other arithmetic  8.39 us (1%)
    ppermute x15, waiting for transfers between devices, shifted(): lax.ppermute(array, axis, [(i, (i + by) % length) for i in range(length)])  477 us
    all_gather x1, blocking collectives, per_device(): gate_whole = lax.all_gather(branch_gate, 'dp', axis=0, tiled=True)  115 us
    all_gather x1, waiting for transfers between devices, per_device(): text_all = lax.all_gather(text_both, 'seq', axis=1, tiled=True)  97.7 us
    ppermute x15, starting transfers between devices, shifted(): lax.ppermute(array, axis, [(i, (i + by) % length) for i in range(length)])  63 us
  transfers between devices with their start and end apart: 17, of which 16 were waited for; matrix products, arithmetic and copies ran while one was open for 1% of the time, Pallas kernels for 0%

commit v1 on v0

v1 whole, which is shorter than its diff:
```python
import functools
import math

import jax
import jax.numpy as jnp
from jax import lax
from jax.experimental import pallas as pl
from jax.experimental.pallas import tpu as pltpu
from jax.sharding import PartitionSpec as P


HEAD_DIM = 128
PLANES = 4
BF16 = jnp.bfloat16
F32 = jnp.float32
VMEM = pl.BlockSpec(memory_space=pltpu.VMEM)
SMEM = pl.BlockSpec(memory_space=pltpu.SMEM)


def place():
    position = lax.axis_index("seq")
    y = lax.div(position, PLANES)
    plane = lax.rem(position, PLANES)
    return y, plane, lax.rem(plane, 2), lax.div(plane, 2)


def move(array, rows, by_y, by_plane):
    pairs = [
        (y * PLANES + z, (y + by_y) % rows * PLANES + (z + by_plane) % PLANES)
        for y in range(rows)
        for z in range(PLANES)
    ]
    return lax.ppermute(array, "seq", pairs)


def swap_cores(array):
    return lax.ppermute(array, "head", [(0, 1), (1, 0)])


def call(body, out_shape, in_specs, cost, limit=24 << 20):
    flops, moved, exps = cost
    return pl.pallas_call(
        body,
        out_shape=out_shape,
        in_specs=in_specs,
        out_specs=jax.tree.map(lambda _: VMEM, out_shape),
        compiler_params=pltpu.CompilerParams(vmem_limit_bytes=limit),
        cost_estimate=pl.CostEstimate(
            flops=flops, bytes_accessed=moved, transcendentals=exps
        ),
    )


def text_body(kt, vt, out):
    text = out.shape[0]
    width = kt.shape[2]
    _, _, sample, _ = place()
    rows = pl.ds(pl.multiple_of((1 - sample) * text, text), text)
    out[:, :width] = kt[0, rows, :]
    out[:, width:] = vt[0, rows, :]


def pack_body(k, v, kt, vt, got, out):
    rows, width = k.shape[1:]
    text = got.shape[0]
    _, _, sample, _ = place()
    mine = pl.ds(pl.multiple_of(sample * text, text), text)
    out[:rows, :width] = k[0]
    out[:rows, width:] = v[0]
    out[rows : rows + text, :width] = kt[0, mine, :]
    out[rows : rows + text, width:] = vt[0, mine, :]
    out[rows + text :, :] = got[...]


def attend_body(kinds, first, last, row_count, *refs):
    live_ref, q_near, q_far = refs[:3]
    refs = refs[3:]
    blocks, refs = refs[: len(kinds)], refs[len(kinds) :]
    if not first:
        acc_in, stat_in = refs[:2]
        refs = refs[2:]
    y, plane, sample, _ = place()
    live = live_ref[0, sample]
    rows, half = q_near.shape[1:]
    heads = half // HEAD_DIM
    width = pl.cdiv(2 * rows, 128) * 128
    factor = math.log2(math.e) / math.sqrt(HEAD_DIM)
    pad = jnp.zeros((width - 2 * rows, HEAD_DIM), BF16)
    logs = []
    for h in range(heads):
        cols = slice(h * HEAD_DIM, (h + 1) * HEAD_DIM)
        vals = slice(half + h * HEAD_DIM, half + (h + 1) * HEAD_DIM)
        queries = jnp.concatenate([q_far[0, :, cols], q_near[0, :, cols], pad], axis=0)
        scores = []
        for (by_y, at), block in zip(kinds, blocks, strict=True):
            s = lax.dot_general(
                block[:, cols], queries, (((1,), (1,)), ((), ())), preferred_element_type=F32
            )
            count = block.shape[0]
            text = at + count - rows
            if text > 0:
                eighth = text // 2
                index = lax.broadcasted_iota(jnp.int32, (text, width), 0)
                origin = lax.rem(plane + lax.div(index, eighth), PLANES)
                slot = (
                    lax.rem(y + by_y, row_count) * (PLANES * eighth)
                    + origin * eighth
                    + lax.rem(index, eighth)
                )
                tail = jnp.where(slot < live, s[count - text :], -1e30)
                s = jnp.concatenate([s[: count - text], tail], axis=0)
            scores.append(s)
        top = functools.reduce(
            jnp.maximum, [jnp.max(s, axis=0, keepdims=True) for s in scores]
        )
        if not first:
            old = stat_in[h : h + 1, :]
            top = jnp.maximum(top, old)
            fade = jnp.exp2((old - top) * factor)
        shift = top * factor
        total = None
        acc = None
        for s, block in zip(scores, blocks, strict=True):
            w = jnp.exp2(s * factor - shift)
            part = jnp.sum(w, axis=0, keepdims=True)
            total = part if total is None else total + part
            out = lax.dot_general(
                block[:, vals],
                w.astype(BF16),
                (((0,), (0,)), ((), ())),
                preferred_element_type=F32,
            )
            acc = out if acc is None else acc + out
        span = slice(h * HEAD_DIM, (h + 1) * HEAD_DIM)
        if not first:
            total = total + fade * stat_in[heads + h : heads + h + 1, :]
            acc = acc + fade * acc_in[span, :]
        if last:
            far_out, near_out, log_out = refs
            result = jnp.transpose(acc / total)
            far_out[:rows, cols] = result[:rows].astype(BF16)
            near_out[:, cols] = result[rows : 2 * rows]
            logs.append(shift + jnp.log2(total))
        else:
            acc_out, stat_out = refs
            acc_out[span, :] = acc
            stat_out[h : h + 1, :] = top
            stat_out[heads + h : heads + h + 1, :] = total
    if last:
        log = jnp.concatenate(logs + [jnp.zeros((8 - heads, width), F32)], axis=0)
        log_out[...] = log
        rest = log
        for n in range(3):
            term = rest.astype(BF16)
            rest = rest - term.astype(F32)
            far_out[rows:, n * 256 : (n + 1) * 256] = term[:, :256]


def attend(row_count, live, q_near, q_far, blocks, state, last):
    rows, half = q_near.shape[1:]
    heads = half // HEAD_DIM
    width = pl.cdiv(2 * rows, 128) * 128
    kinds = tuple((by_y, at) for _, by_y, at in blocks)
    if last:
        out_shape = (
            jax.ShapeDtypeStruct((rows + 8, half), BF16),
            jax.ShapeDtypeStruct((rows, half), F32),
            jax.ShapeDtypeStruct((8, width), F32),
        )
    else:
        out_shape = (
            jax.ShapeDtypeStruct((half, width), F32),
            jax.ShapeDtypeStruct((16, width), F32),
        )
    keys = sum(b.shape[0] for b, _, _ in blocks)
    args = [live, q_near, q_far] + [b for b, _, _ in blocks] + list(state or ())
    return call(
        functools.partial(attend_body, kinds, state is None, last, row_count),
        out_shape,
        [SMEM] + [VMEM] * (len(args) - 1),
        (4 * keys * width * half, sum(a.size * 2 for a in args), keys * width * heads),
    )(*args)


def merge_body(got, near, log, out):
    rows, half = near.shape
    terms = [got[rows:, n * 256 : (n + 1) * 256].astype(F32) for n in range(3)]
    theirs = jnp.transpose(terms[0] + terms[1] + terms[2])
    mine = jnp.transpose(log[...])
    for h in range(half // HEAD_DIM):
        cols = slice(h * HEAD_DIM, (h + 1) * HEAD_DIM)
        a = mine[rows : 2 * rows, h : h + 1]
        b = theirs[:rows, h : h + 1]
        share = 1.0 / (1.0 + jnp.exp2(jnp.minimum(b - a, 126.0)))
        out[:, cols] = (
            near[:, cols] * share + got[:rows, cols].astype(F32) * (1.0 - share)
        ).astype(BF16)


def project_first_body(mine, w_own, out):
    out[...] = jnp.dot(mine[...], w_own[...], preferred_element_type=F32)


def project_last_body(x_size, partial, theirs, w_got, gates, out):
    total = partial[...] + jnp.dot(theirs[...], w_got[...], preferred_element_type=F32)
    blocks, _, gate_width = gates.shape
    z_size = blocks // x_size
    me = lax.axis_index("dp")
    first = lax.axis_index("head") * (blocks // 2)
    for j in range(blocks // 2):
        by_x = lax.rem(lax.rem(me, x_size) - lax.rem(first + j, x_size) + x_size, x_size)
        by_z = lax.rem(lax.div(me, x_size) - lax.div(first + j, x_size) + z_size, z_size)
        cols = slice(j * gate_width, (j + 1) * gate_width)
        out[0, :, cols] = (total[:, cols] * gates[by_z * x_size + by_x]).astype(BF16)


def gather_gates(gate, x_size, z_size):
    def along(array, by_z, by_x):
        pairs = [
            (z * x_size + x, (z + by_z) % z_size * x_size + (x + by_x) % x_size)
            for z in range(z_size)
            for x in range(x_size)
        ]
        return lax.ppermute(array, "dp", pairs)

    held = gate.reshape(1, 1, gate.shape[0])
    step = 1
    while step < x_size:
        held = jnp.concatenate([held, along(held, 0, step)], axis=0)
        step *= 2
    return jnp.concatenate([held] + [along(held, i, 0) for i in range(1, z_size)], axis=0)


def per_device(q_img, k_img, v_img, k_txt, v_txt, text_length, w_out, branch_gate):
    row_count = lax.axis_size("seq") // PLANES
    rows, width = q_img.shape[1:]
    text = k_txt.shape[1] // 2

    def shape(*dims):
        return jax.ShapeDtypeStruct(dims, BF16)

    t_send = call(
        text_body, shape(text, 2 * width), [VMEM] * 2, (0, 8 * text * width, 0)
    )(k_txt, v_txt)
    t_got = move(t_send, row_count, 0, -1)
    block = call(
        pack_body, shape(rows + 2 * text, 2 * width), [VMEM] * 5, (0, 8 * rows * width, 0)
    )(k_img, v_img, k_txt, v_txt, t_got)
    q_got = move(q_img, row_count, 0, 2)

    up, down = [block], [block]
    for _ in range(1, 4):
        up.append(move(up[-1], row_count, 1, 0))
        down.append(move(down[-1], row_count, -1, 0))
    cut = (rows + 2 * text) // 2
    up.append(move(up[3][:cut], row_count, 1, 0))
    down.append(move(down[3][cut:], row_count, -1, 0))

    groups = [
        [(block, 0, 0), (up[1], -1, 0), (down[1], 1, 0)],
        [(up[2], -2, 0), (down[2], 2, 0)],
        [(up[3], -3, 0), (down[3], 3, 0)],
        [(up[4], -4, 0), (down[4], 4, cut)],
    ]
    state = None
    for n, group in enumerate(groups):
        blocks = [(b, by % row_count, at) for b, by, at in group]
        state = attend(row_count, text_length, q_img, q_got, blocks, state, n == len(groups) - 1)
    o_far, o_near, o_log = state

    core = lax.axis_index("head")
    out_width = w_out.shape[1] // 2
    w_send = lax.dynamic_slice_in_dim(w_out, (1 - core) * out_width, out_width, 1)
    w_own = lax.dynamic_slice_in_dim(w_out, core * out_width, out_width, 1)
    w_got = swap_cores(w_send)
    gates = gather_gates(branch_gate, 4, lax.axis_size("dp") // 4)

    o_got = move(o_far, row_count, 0, 2)
    mine = call(
        merge_body, shape(rows, width), [VMEM] * 3, (0, 8 * rows * width, 0)
    )(o_got, o_near, o_log)
    theirs = swap_cores(mine)
    partial = call(
        project_first_body,
        jax.ShapeDtypeStruct((rows, out_width), F32),
        [VMEM] * 2,
        (2 * rows * width * out_width, 2 * width * out_width, 0),
    )(mine, w_own)
    return call(
        functools.partial(project_last_body, 4),
        shape(1, rows, out_width),
        [VMEM] * 4,
        (2 * rows * width * out_width, 2 * width * out_width, 0),
    )(partial, theirs, w_got, gates)


def solution(mesh):
    in_specs = (
        P("dp", "seq", "head"),
        P("dp", "seq", "head"),
        P("dp", "seq", "head"),
        P("dp", "seq", "head"),
        P("dp", "seq", "head"),
        P("dp", None),
        P("head", None),
        P("dp"),
    )
    out_specs = P("dp", "seq", "head")
    return jax.shard_map(
        per_device, mesh=mesh, in_specs=in_specs, out_specs=out_specs, check_vma=False
    )
```

time: 816 us -> 125 us (0.15)
  the two profiles are of different devices: /device:TPU:138 before, /device:TPU:1 now
where the time goes in v1:
time: 125 us
  starting transfers between devices  85.3 us (68%)
  waiting for transfers between devices  17.8 us (14%)
  Pallas kernels  14.9 us (12%)
  local copies, waits for them, and re-layouts  6.2 us (5%)
    ppermute x11, starting transfers between devices, move(): return lax.ppermute(array, 'seq', pairs)  57 us
    ppermute x4, starting transfers between devices, along(): return lax.ppermute(array, 'dp', pairs)  19.1 us
    ppermute x11, waiting for transfers between devices, move(): return lax.ppermute(array, 'seq', pairs)  15.8 us
    pallas_call x4, Pallas kernels, attend(): call(functools.partial(attend_body, kinds, state is None, last, row_count...  12.4 us
    ppermute x2, starting transfers between devices, swap_cores(): return lax.ppermute(array, 'head', [(0, 1), (1, 0)])  9.24 us
    unnamed x18, local copies, waits for them, and re-layouts  3.43 us
    dynamic_slice x1, local copies, waits for them, and re-layouts, per_device(): lax.dynamic_slice_in_dim(w_out, (1 - core) * out_width, out_width, 1)  2.72 us
  transfers between devices with their start and end apart: 17, of which 6 were waited for; matrix products, arithmetic and copies ran while one was open for 2% of the time, Pallas kernels for 11%

profile of v1, /device:TPU:1, one launch (start us, length us, event | category | flops | bytes accessed | tf_op | source)
XLA Modules:
  0.0 124.7 jit_solution(7598813634933370187)
XLA Ops:
  0.0 0.7 copy-done.3
  0.7 0.7 copy-done.4
  1.5 15.1 %collective-permute-start.1 = (bf16[8,1536]{1,0:T(8,128)(2,1)S(1)}, bf16[8,1536]{1,0:T(8,128)(2,1)S(1)}, u32[]{:S(2)}, u32[]{:S(2)}) collective-permute-start(bf16[8,1536]{1,0:T(8,128)(2,1)S(1)} %shard_map.82), channel_id=1, source_target_pairs={{0,6},{2,0},{4,2},{6,4},{8,14},{10,8},{12,10},{14,12},{16,22},{18,... | collective-permute-start | bytes 73736 | tf_op jit(solution)/shard_map/ppermute | solution.py:33
  16.6 0.9 collective-permute-done.1.got
  17.5 1.0 copy-done.1
  18.5 1.0 copy-done.2
  19.5 3.2 %collective-permute-start.2 = (bf16[192,1536]{1,0:T(8,128)(2,1)S(1)}, bf16[192,1536]{1,0:T(8,128)(2,1)S(1)}, u32[]{:S(2)}, u32[]{:S(2)}) collective-permute-start(bf16[192,1536]{1,0:T(8,128)(2,1)S(1)} %shard_map.83.refs_3_), channel_id=1, source_target_pairs={{0,8},{2,10},{4,12},{6,14},{8,16},{10,18},{12,20},{14,22},{16,24},... | collective-permute-start | bytes 1769480 | tf_op jit(solution)/shard_map/ppermute | solution.py:33
  22.7 3.8 %collective-permute-start.6 = (bf16[192,1536]{1,0:T(8,128)(2,1)S(1)}, bf16[192,1536]{1,0:T(8,128)(2,1)S(1)}, u32[]{:S(2)}, u32[]{:S(2)}) collective-permute-start(bf16[192,1536]{1,0:T(8,128)(2,1)S(1)} %shard_map.83.refs_3_), channel_id=1, source_target_pairs={{0,56},{2,58},{4,60},{6,62},{8,0},{10,2},{12,4},{14,6},{16,8},{18,... | collective-permute-start | bytes 1769480 | tf_op jit(solution)/shard_map/ppermute | solution.py:33
  26.5 0.0 copy-start
  26.5 0.0 copy-start.6
  26.5 0.0 copy-start.5
  26.5 2.7 %constant_dynamic-slice_fusion = (bf16[768,1536]{1,0:T(8,128)(2,1)S(1)}, bf16[768,1536]{1,0:T(8,128)(2,1)S(1)}) fusion(bf16[768,3072]{1,0:T(8,128)(2,1)} %param.14, s32[]{:T(128)S(6)} %select_n.7, s32[]{:T(128)S(6)} %select_n.6), kind=kLoop, calls=%fused_computation.7 | loop fusion | bytes 9437192 | tf_op jit(solution)/shard_map/dynamic_slice | solution.py:273
  29.3 3.9 %collective-permute-start.12 = (bf16[768,1536]{1,0:T(8,128)(2,1)S(1)}, bf16[768,1536]{1,0:T(8,128)(2,1)S(1)}, u32[]{:S(2)}, u32[]{:S(2)}) collective-permute-start(bf16[768,1536]{1,0:T(8,128)(2,1)S(1)} %get-tuple-element.23), channel_id=1, source_target_pairs={{0,1},{1,0},{2,3},{3,2},{4,5},{5,4},{6,7},{7,6},{8,9},{9,8},{10,11... | collective-permute-start | bytes 7077896 | tf_op jit(solution)/shard_map/ppermute | solution.py:37
  33.2 3.4 %collective-permute-done.2.refs_4_ = bf16[192,1536]{1,0:T(8,128)(2,1)S(1)} collective-permute-done((bf16[192,1536]{1,0:T(8,128)(2,1)S(1)}, bf16[192,1536]{1,0:T(8,128)(2,1)S(1)}, u32[]{:S(2)}, u32[]{:S(2)}) %collective-permute-start.2) | collective-permute-done | bytes 589856 | tf_op jit(solution)/shard_map/ppermute | solution.py:33
  36.5 1.9 %collective-permute-start.3 = (bf16[192,1536]{1,0:T(8,128)(2,1)S(1)}, bf16[192,1536]{1,0:T(8,128)(2,1)S(1)}, u32[]{:S(2)}, u32[]{:S(2)}) collective-permute-start(bf16[192,1536]{1,0:T(8,128)(2,1)S(1)} %collective-permute-done.2.refs_4_), channel_id=1, source_target_pairs={{0,8},{2,10},{4,12},{6,14},{8,16},{10,18},{12,20},{14,22},{16,24},... | collective-permute-start | bytes 1769480 | tf_op jit(solution)/shard_map/ppermute | solution.py:33
  38.4 0.0 collective-permute-done.6.refs_5_
  38.5 4.6 %collective-permute-start.7 = (bf16[192,1536]{1,0:T(8,128)(2,1)S(1)}, bf16[192,1536]{1,0:T(8,128)(2,1)S(1)}, u32[]{:S(2)}, u32[]{:S(2)}) collective-permute-start(bf16[192,1536]{1,0:T(8,128)(2,1)S(1)} %collective-permute-done.6.refs_5_), channel_id=1, source_target_pairs={{0,56},{2,58},{4,60},{6,62},{8,0},{10,2},{12,4},{14,6},{16,8},{18,... | collective-permute-start | bytes 1769480 | tf_op jit(solution)/shard_map/ppermute | solution.py:33
  43.0 9.2 %collective-permute-done.3.refs_3_ = bf16[192,1536]{1,0:T(8,128)(2,1)S(1)} collective-permute-done((bf16[192,1536]{1,0:T(8,128)(2,1)S(1)}, bf16[192,1536]{1,0:T(8,128)(2,1)S(1)}, u32[]{:S(2)}, u32[]{:S(2)}) %collective-permute-start.3) | collective-permute-done | bytes 589856 | tf_op jit(solution)/shard_map/ppermute | solution.py:33
  52.2 1.9 %collective-permute-start.4 = (bf16[192,1536]{1,0:T(8,128)(2,1)S(1)}, bf16[192,1536]{1,0:T(8,128)(2,1)S(1)}, u32[]{:S(2)}, u32[]{:S(2)}) collective-permute-start(bf16[192,1536]{1,0:T(8,128)(2,1)S(1)} %collective-permute-done.3.refs_3_), channel_id=1, source_target_pairs={{0,8},{2,10},{4,12},{6,14},{8,16},{10,18},{12,20},{14,22},{16,24},... | collective-permute-start | bytes 1769480 | tf_op jit(solution)/shard_map/ppermute | solution.py:33
  54.1 0.0 collective-permute-done.7.refs_4_
  54.1 4.6 %collective-permute-start.8 = (bf16[192,1536]{1,0:T(8,128)(2,1)S(1)}, bf16[192,1536]{1,0:T(8,128)(2,1)S(1)}, u32[]{:S(2)}, u32[]{:S(2)}) collective-permute-start(bf16[192,1536]{1,0:T(8,128)(2,1)S(1)} %collective-permute-done.7.refs_4_), channel_id=1, source_target_pairs={{0,56},{2,58},{4,60},{6,62},{8,0},{10,2},{12,4},{14,6},{16,8},{18,... | collective-permute-start | bytes 1769480 | tf_op jit(solution)/shard_map/ppermute | solution.py:33
  58.7 6.0 %collective-permute-start = (bf16[1,176,768]{2,1,0:T(8,128)(2,1)S(1)}, bf16[1,176,768]{2,1,0:T(8,128)(2,1)S(1)}, u32[]{:S(2)}, u32[]{:S(2)}) collective-permute-start(bf16[1,176,768]{2,1,0:T(8,128)(2,1)S(1)} %copy-done), channel_id=1, source_target_pairs={{0,4},{2,6},{4,0},{6,2},{8,12},{10,14},{12,8},{14,10},{16,20},{18,... | collective-permute-start | bytes 811016 | tf_op jit(solution)/shard_map/ppermute | solution.py:33
  64.7 2.3 %collective-permute-done.4.refs_3_ = bf16[192,1536]{1,0:T(8,128)(2,1)S(1)} collective-permute-done((bf16[192,1536]{1,0:T(8,128)(2,1)S(1)}, bf16[192,1536]{1,0:T(8,128)(2,1)S(1)}, u32[]{:S(2)}, u32[]{:S(2)}) %collective-permute-start.4) | collective-permute-done | bytes 589856 | tf_op jit(solution)/shard_map/ppermute | solution.py:33
  67.1 1.9 %collective-permute-start.5 = (bf16[96,1536]{1,0:T(8,128)(2,1)S(1)}, bf16[96,1536]{1,0:T(8,128)(2,1)S(1)}, u32[]{:S(2)}, u32[]{:S(2)}) collective-permute-start(bf16[96,1536]{1,0:T(8,128)(2,1)S(1)} %slice.8), channel_id=1, source_target_pairs={{0,8},{2,10},{4,12},{6,14},{8,16},{10,18},{12,20},{14,22},{16,24},... | collective-permute-start | bytes 884744 | tf_op jit(solution)/shard_map/ppermute | solution.py:33
  69.0 0.0 collective-permute-done.8.refs_4_
  69.0 4.6 %collective-permute-start.9 = (bf16[96,1536]{1,0:T(8,128)(2,1)S(1)}, bf16[96,1536]{1,0:T(8,128)(2,1)S(1)}, u32[]{:S(2)}, u32[]{:S(2)}) collective-permute-start(bf16[96,1536]{1,0:T(8,128)(2,1)S(1)} %slice.9), channel_id=1, source_target_pairs={{0,56},{2,58},{4,60},{6,62},{8,0},{10,2},{12,4},{14,6},{16,8},{18,... | collective-permute-start | bytes 884744 | tf_op jit(solution)/shard_map/ppermute | solution.py:33
  73.6 3.7 %collective-permute-start.13 = (f32[1,1,256]{2,1,0:T(1,128)S(1)}, f32[1,1,256]{2,1,0:T(1,128)S(1)}, u32[]{:S(2)}, u32[]{:S(2)}) collective-permute-start(f32[1,1,256]{2,1,0:T(1,128)S(1)} %bitcast.1), channel_id=1, source_target_pairs={{0,64},{64,128},{128,192},{192,0},{256,320},{320,384},{384,448},{4... | collective-permute-start | bytes 3080 | tf_op jit(solution)/shard_map/ppermute | solution.py:224
  77.3 0.0 collective-permute-done.refs_2_
  77.4 3.8 %shard_map.84 = (f32[768,384]{1,0:T(8,128)S(1)}, f32[16,384]{1,0:T(8,128)S(1)}) custom-call(s32[1,2]{1,0:T(1,128)S(1)} %copy-done.5, bf16[1,176,768]{2,1,0:T(8,128)(2,1)S(1)} %copy-done, bf16[1,176,768]{2,1,0:T(8,128)(2,1)S(1)} %collective-permute-done.refs_2_, bf16[192,1536]{1,0:T(8,128)(2,1)S(1)} %shard_map.83.refs_3_, ...), custom_call_target="tpu_custom_call" | custom-call | flops 679477248 | bytes 2310148 | tf_op jit(solution)/shard_map/pallas_call | solution.py:177
  81.1 3.1 %shard_map.85 = (f32[768,384]{1,0:T(8,128)S(1)}, f32[16,384]{1,0:T(8,128)S(1)}) custom-call(s32[1,2]{1,0:T(1,128)S(1)} %copy-done.5, bf16[1,176,768]{2,1,0:T(8,128)(2,1)S(1)} %copy-done, bf16[1,176,768]{2,1,0:T(8,128)(2,1)S(1)} %collective-permute-done.refs_2_, bf16[192,1536]{1,0:T(8,128)(2,1)S(1)} %collective-permute-done.3.refs_3_, ...), custom_call_target="tpu_custom_call" | custom-call | flops 452984832 | bytes 2322436 | tf_op jit(solution)/shard_map/pallas_call | solution.py:177
  84.2 3.1 %shard_map.86 = (f32[768,384]{1,0:T(8,128)S(1)}, f32[16,384]{1,0:T(8,128)S(1)}) custom-call(s32[1,2]{1,0:T(1,128)S(1)} %copy-done.5, bf16[1,176,768]{2,1,0:T(8,128)(2,1)S(1)} %copy-done, bf16[1,176,768]{2,1,0:T(8,128)(2,1)S(1)} %collective-permute-done.refs_2_, bf16[192,1536]{1,0:T(8,128)(2,1)S(1)} %collective-permute-done.4.refs_3_, ...), custom_call_target="tpu_custom_call" | custom-call | flops 452984832 | bytes 2322436 | tf_op jit(solution)/shard_map/pallas_call | solution.py:177
  87.3 0.0 collective-permute-done.5.refs_3_
  87.3 0.0 collective-permute-done.9.refs_4_
  87.3 2.5 %shard_map.87 = (bf16[184,768]{1,0:T(8,128)(2,1)S(1)}, f32[176,768]{1,0:T(8,128)S(1)}, f32[8,384]{1,0:T(8,128)S(1)}) custom-call(s32[1,2]{1,0:T(1,128)S(1)} %copy-done.5, bf16[1,176,768]{2,1,0:T(8,128)(2,1)S(1)} %copy-done, bf16[1,176,768]{2,1,0:T(8,128)(2,1)S(1)} %collective-permute-done.refs_2_, bf16[96,1536]{1,0:T(8,128)(2,1)S(1)} %collective-permute-done.5.refs_3_, ...), custom_call_target="tpu_custom_call" | custom-call | flops 226492416 | bytes 1732612 | tf_op jit(solution)/shard_map/pallas_call | solution.py:177
  89.8 9.4 %collective-permute-start.10 = (bf16[184,768]{1,0:T(8,128)(2,1)S(1)}, bf16[184,768]{1,0:T(8,128)(2,1)S(1)}, u32[]{:S(2)}, u32[]{:S(2)}) collective-permute-start(bf16[184,768]{1,0:T(8,128)(2,1)S(1)} %get-tuple-element.20), channel_id=1, source_target_pairs={{0,4},{2,6},{4,0},{6,2},{8,12},{10,14},{12,8},{14,10},{16,20},{18,... | collective-permute-start | bytes 847880 | tf_op jit(solution)/shard_map/ppermute | solution.py:33
  99.3 0.0 collective-permute-done.13
  99.3 4.3 %collective-permute-start.14 = (f32[2,1,256]{2,1,0:T(1,128)S(1)}, f32[2,1,256]{2,1,0:T(1,128)S(1)}, u32[]{:S(2)}, u32[]{:S(2)}) collective-permute-start(f32[2,1,256]{2,1,0:T(1,128)S(1)} %pad_maximum_fusion.1), channel_id=1, source_target_pairs={{0,128},{64,192},{128,0},{192,64},{256,384},{320,448},{384,256},{4... | collective-permute-start | bytes 6152 | tf_op jit(solution)/shard_map/ppermute | solution.py:224
  103.6 1.5 %collective-permute-done.14 = f32[2,1,256]{2,1,0:T(1,128)S(1)} collective-permute-done((f32[2,1,256]{2,1,0:T(1,128)S(1)}, f32[2,1,256]{2,1,0:T(1,128)S(1)}, u32[]{:S(2)}, u32[]{:S(2)}) %collective-permute-start.14) | collective-permute-done | bytes 2080 | tf_op jit(solution)/shard_map/ppermute | solution.py:224
  105.1 8.7 %collective-permute-start.15 = (f32[4,1,256]{2,1,0:T(1,128)S(1)}, f32[4,1,256]{2,1,0:T(1,128)S(1)}, u32[]{:S(2)}, u32[]{:S(2)}) collective-permute-start(f32[4,1,256]{2,1,0:T(1,128)S(1)} %pad_maximum_fusion), channel_id=1, source_target_pairs={{0,256},{64,320},{128,384},{192,448},{256,512},{320,576},{384,640}... | collective-permute-start | bytes 12296 | tf_op jit(solution)/shard_map/ppermute | solution.py:224
  113.9 2.4 %collective-permute-start.16 = (f32[4,1,256]{2,1,0:T(1,128)S(1)}, f32[4,1,256]{2,1,0:T(1,128)S(1)}, u32[]{:S(2)}, u32[]{:S(2)}) collective-permute-start(f32[4,1,256]{2,1,0:T(1,128)S(1)} %pad_maximum_fusion), channel_id=1, source_target_pairs={{0,512},{64,576},{128,640},{192,704},{256,0},{320,64},{384,128},{4... | collective-permute-start | bytes 12296 | tf_op jit(solution)/shard_map/ppermute | solution.py:224
  116.3 0.0 collective-permute-done.10.got
  116.3 0.5 shard_map.88.mine
  116.8 5.3 %collective-permute-start.11 = (bf16[176,768]{1,0:T(8,128)(2,1)S(1)}, bf16[176,768]{1,0:T(8,128)(2,1)S(1)}, u32[]{:S(2)}, u32[]{:S(2)}) collective-permute-start(bf16[176,768]{1,0:T(8,128)(2,1)S(1)} %shard_map.88.mine), channel_id=1, source_target_pairs={{0,1},{1,0},{2,3},{3,2},{4,5},{5,4},{6,7},{7,6},{8,9},{9,8},{10,11... | collective-permute-start | bytes 811016 | tf_op jit(solution)/shard_map/ppermute | solution.py:37
  122.1 0.0 collective-permute-done.16
  122.2 0.6 shard_map.89.partial
  122.8 0.0 collective-permute-done.12.w_got
  122.8 0.5 collective-permute-done.11.theirs
  123.3 1.4 %shard_map.90 = bf16[1,176,1536]{2,1,0:T(8,128)(2,1)} custom-call(f32[176,1536]{1,0:T(8,128)S(1)} %shard_map.89.partial, bf16[176,768]{1,0:T(8,128)(2,1)S(1)} %collective-permute-done.11.theirs, bf16[768,1536]{1,0:T(8,128)(2,1)S(1)} %collective-permute-done.12.w_got, f32[12,1,256]{2,1,0:T(1,128)S(1)} %constant_dynamic-update-slice_fusion.gates), custom_call_target="tpu_custom_call" | custom-call | flops 415236096 | bytes 2359296 | tf_op jit(solution)/shard_map/pallas_call | solution.py:289
  (19 shorter events, 0.1 us)
Async XLA Ops:
  0.0 0.7 copy-start.3
  0.7 0.7 copy-start.4
  1.5 16.0 %collective-permute-start.1 = (bf16[8,1536]{1,0:T(8,128)(2,1)S(1)}, bf16[8,1536]{1,0:T(8,128)(2,1)S(1)}, u32[]{:S(2)}, u32[]{:S(2)}) collective-permute-start(bf16[8,1536]{1,0:T(8,128)(2,1)S(1)} %shard_map.82), channel_id=1, source_target_pairs={{0,6},{2,0},{4,2},{6,4},{8,14},{10,8},{12,10},{14,12},{16,22},{18,... | collective-permute-start | bytes 73736 | tf_op jit(solution)/shard_map/ppermute | solution.py:33
  17.5 1.0 copy-start.1
  18.5 1.0 copy-start.2
  19.5 17.1 %collective-permute-start.2 = (bf16[192,1536]{1,0:T(8,128)(2,1)S(1)}, bf16[192,1536]{1,0:T(8,128)(2,1)S(1)}, u32[]{:S(2)}, u32[]{:S(2)}) collective-permute-start(bf16[192,1536]{1,0:T(8,128)(2,1)S(1)} %shard_map.83.refs_3_), channel_id=1, source_target_pairs={{0,8},{2,10},{4,12},{6,14},{8,16},{10,18},{12,20},{14,22},{16,24},... | collective-permute-start | bytes 1769480 | tf_op jit(solution)/shard_map/ppermute | solution.py:33
  22.7 15.8 %collective-permute-start.6 = (bf16[192,1536]{1,0:T(8,128)(2,1)S(1)}, bf16[192,1536]{1,0:T(8,128)(2,1)S(1)}, u32[]{:S(2)}, u32[]{:S(2)}) collective-permute-start(bf16[192,1536]{1,0:T(8,128)(2,1)S(1)} %shard_map.83.refs_3_), channel_id=1, source_target_pairs={{0,56},{2,58},{4,60},{6,62},{8,0},{10,2},{12,4},{14,6},{16,8},{18,... | collective-permute-start | bytes 1769480 | tf_op jit(solution)/shard_map/ppermute | solution.py:33
  26.5 32.2 %copy-start = (bf16[1,176,768]{2,1,0:T(8,128)(2,1)S(1)}, bf16[1,176,768]{2,1,0:T(8,128)(2,1)}, u32[]{:S(2)}) copy-start(bf16[1,176,768]{2,1,0:T(8,128)(2,1)} %refs_1_.7) | copy-start | bytes 811012
  26.5 47.1 %copy-start.6 = (f32[256]{0:T(256)S(1)}, f32[256]{0:T(256)}, u32[]{:S(2)}) copy-start(f32[256]{0:T(256)} %param.15) | copy-start | bytes 3076
  26.5 50.8 %copy-start.5 = (s32[1,2]{1,0:T(1,128)S(1)}, s32[1,2]{1,0:T(1,128)}, u32[]{:S(2)}) copy-start(s32[1,2]{1,0:T(1,128)} %refs_0_.7) | copy-start | bytes 28
  29.3 93.5 %collective-permute-start.12 = (bf16[768,1536]{1,0:T(8,128)(2,1)S(1)}, bf16[768,1536]{1,0:T(8,128)(2,1)S(1)}, u32[]{:S(2)}, u32[]{:S(2)}) collective-permute-start(bf16[768,1536]{1,0:T(8,128)(2,1)S(1)} %get-tuple-element.23), channel_id=1, source_target_pairs={{0,1},{1,0},{2,3},{3,2},{4,5},{5,4},{6,7},{7,6},{8,9},{9,8},{10,11... | collective-permute-start | bytes 7077896 | tf_op jit(solution)/shard_map/ppermute | solution.py:37
  36.5 15.7 %collective-permute-start.3 = (bf16[192,1536]{1,0:T(8,128)(2,1)S(1)}, bf16[192,1536]{1,0:T(8,128)(2,1)S(1)}, u32[]{:S(2)}, u32[]{:S(2)}) collective-permute-start(bf16[192,1536]{1,0:T(8,128)(2,1)S(1)} %collective-permute-done.2.refs_4_), channel_id=1, source_target_pairs={{0,8},{2,10},{4,12},{6,14},{8,16},{10,18},{12,20},{14,22},{16,24},... | collective-permute-start | bytes 1769480 | tf_op jit(solution)/shard_map/ppermute | solution.py:33
  38.5 15.7 %collective-permute-start.7 = (bf16[192,1536]{1,0:T(8,128)(2,1)S(1)}, bf16[192,1536]{1,0:T(8,128)(2,1)S(1)}, u32[]{:S(2)}, u32[]{:S(2)}) collective-permute-start(bf16[192,1536]{1,0:T(8,128)(2,1)S(1)} %collective-permute-done.6.refs_5_), channel_id=1, source_target_pairs={{0,56},{2,58},{4,60},{6,62},{8,0},{10,2},{12,4},{14,6},{16,8},{18,... | collective-permute-start | bytes 1769480 | tf_op jit(solution)/shard_map/ppermute | solution.py:33
  52.2 14.8 %collective-permute-start.4 = (bf16[192,1536]{1,0:T(8,128)(2,1)S(1)}, bf16[192,1536]{1,0:T(8,128)(2,1)S(1)}, u32[]{:S(2)}, u32[]{:S(2)}) collective-permute-start(bf16[192,1536]{1,0:T(8,128)(2,1)S(1)} %collective-permute-done.3.refs_3_), channel_id=1, source_target_pairs={{0,8},{2,10},{4,12},{6,14},{8,16},{10,18},{12,20},{14,22},{16,24},... | collective-permute-start | bytes 1769480 | tf_op jit(solution)/shard_map/ppermute | solution.py:33
  54.1 14.9 %collective-permute-start.8 = (bf16[192,1536]{1,0:T(8,128)(2,1)S(1)}, bf16[192,1536]{1,0:T(8,128)(2,1)S(1)}, u32[]{:S(2)}, u32[]{:S(2)}) collective-permute-start(bf16[192,1536]{1,0:T(8,128)(2,1)S(1)} %collective-permute-done.7.refs_4_), channel_id=1, source_target_pairs={{0,56},{2,58},{4,60},{6,62},{8,0},{10,2},{12,4},{14,6},{16,8},{18,... | collective-permute-start | bytes 1769480 | tf_op jit(solution)/shard_map/ppermute | solution.py:33
  58.7 18.6 %collective-permute-start = (bf16[1,176,768]{2,1,0:T(8,128)(2,1)S(1)}, bf16[1,176,768]{2,1,0:T(8,128)(2,1)S(1)}, u32[]{:S(2)}, u32[]{:S(2)}) collective-permute-start(bf16[1,176,768]{2,1,0:T(8,128)(2,1)S(1)} %copy-done), channel_id=1, source_target_pairs={{0,4},{2,6},{4,0},{6,2},{8,12},{10,14},{12,8},{14,10},{16,20},{18,... | collective-permute-start | bytes 811016 | tf_op jit(solution)/shard_map/ppermute | solution.py:33
  67.1 20.2 %collective-permute-start.5 = (bf16[96,1536]{1,0:T(8,128)(2,1)S(1)}, bf16[96,1536]{1,0:T(8,128)(2,1)S(1)}, u32[]{:S(2)}, u32[]{:S(2)}) collective-permute-start(bf16[96,1536]{1,0:T(8,128)(2,1)S(1)} %slice.8), channel_id=1, source_target_pairs={{0,8},{2,10},{4,12},{6,14},{8,16},{10,18},{12,20},{14,22},{16,24},... | collective-permute-start | bytes 884744 | tf_op jit(solution)/shard_map/ppermute | solution.py:33
  69.0 18.3 %collective-permute-start.9 = (bf16[96,1536]{1,0:T(8,128)(2,1)S(1)}, bf16[96,1536]{1,0:T(8,128)(2,1)S(1)}, u32[]{:S(2)}, u32[]{:S(2)}) collective-permute-start(bf16[96,1536]{1,0:T(8,128)(2,1)S(1)} %slice.9), channel_id=1, source_target_pairs={{0,56},{2,58},{4,60},{6,62},{8,0},{10,2},{12,4},{14,6},{16,8},{18,... | collective-permute-start | bytes 884744 | tf_op jit(solution)/shard_map/ppermute | solution.py:33
  73.6 25.7 %collective-permute-start.13 = (f32[1,1,256]{2,1,0:T(1,128)S(1)}, f32[1,1,256]{2,1,0:T(1,128)S(1)}, u32[]{:S(2)}, u32[]{:S(2)}) collective-permute-start(f32[1,1,256]{2,1,0:T(1,128)S(1)} %bitcast.1), channel_id=1, source_target_pairs={{0,64},{64,128},{128,192},{192,0},{256,320},{320,384},{384,448},{4... | collective-permute-start | bytes 3080 | tf_op jit(solution)/shard_map/ppermute | solution.py:224
  89.8 26.5 %collective-permute-start.10 = (bf16[184,768]{1,0:T(8,128)(2,1)S(1)}, bf16[184,768]{1,0:T(8,128)(2,1)S(1)}, u32[]{:S(2)}, u32[]{:S(2)}) collective-permute-start(bf16[184,768]{1,0:T(8,128)(2,1)S(1)} %get-tuple-element.20), channel_id=1, source_target_pairs={{0,4},{2,6},{4,0},{6,2},{8,12},{10,14},{12,8},{14,10},{16,20},{18,... | collective-permute-start | bytes 847880 | tf_op jit(solution)/shard_map/ppermute | solution.py:33
  99.3 5.8 %collective-permute-start.14 = (f32[2,1,256]{2,1,0:T(1,128)S(1)}, f32[2,1,256]{2,1,0:T(1,128)S(1)}, u32[]{:S(2)}, u32[]{:S(2)}) collective-permute-start(f32[2,1,256]{2,1,0:T(1,128)S(1)} %pad_maximum_fusion.1), channel_id=1, source_target_pairs={{0,128},{64,192},{128,0},{192,64},{256,384},{320,448},{384,256},{4... | collective-permute-start | bytes 6152 | tf_op jit(solution)/shard_map/ppermute | solution.py:224
  105.1 17.0 %collective-permute-start.15 = (f32[4,1,256]{2,1,0:T(1,128)S(1)}, f32[4,1,256]{2,1,0:T(1,128)S(1)}, u32[]{:S(2)}, u32[]{:S(2)}) collective-permute-start(f32[4,1,256]{2,1,0:T(1,128)S(1)} %pad_maximum_fusion), channel_id=1, source_target_pairs={{0,256},{64,320},{128,384},{192,448},{256,512},{320,576},{384,640}... | collective-permute-start | bytes 12296 | tf_op jit(solution)/shard_map/ppermute | solution.py:224
  113.9 8.3 %collective-permute-start.16 = (f32[4,1,256]{2,1,0:T(1,128)S(1)}, f32[4,1,256]{2,1,0:T(1,128)S(1)}, u32[]{:S(2)}, u32[]{:S(2)}) collective-permute-start(f32[4,1,256]{2,1,0:T(1,128)S(1)} %pad_maximum_fusion), channel_id=1, source_target_pairs={{0,512},{64,576},{128,640},{192,704},{256,0},{320,64},{384,128},{4... | collective-permute-start | bytes 12296 | tf_op jit(solution)/shard_map/ppermute | solution.py:224
  116.8 6.5 %collective-permute-start.11 = (bf16[176,768]{1,0:T(8,128)(2,1)S(1)}, bf16[176,768]{1,0:T(8,128)(2,1)S(1)}, u32[]{:S(2)}, u32[]{:S(2)}) collective-permute-start(bf16[176,768]{1,0:T(8,128)(2,1)S(1)} %shard_map.88.mine), channel_id=1, source_target_pairs={{0,1},{1,0},{2,3},{3,2},{4,5},{5,4},{6,7},{7,6},{8,9},{9,8},{10,11... | collective-permute-start | bytes 811016 | tf_op jit(solution)/shard_map/ppermute | solution.py:37

commit v2 on v1

--- a/solution.py
+++ b/solution.py
@@ -15,6 +15,7 @@
 F32 = jnp.float32
 VMEM = pl.BlockSpec(memory_space=pltpu.VMEM)
 SMEM = pl.BlockSpec(memory_space=pltpu.SMEM)
+ANY = pl.BlockSpec(memory_space=pl.ANY)
 
 
 def place():
@@ -37,13 +38,14 @@
     return lax.ppermute(array, "head", [(0, 1), (1, 0)])
 
 
-def call(body, out_shape, in_specs, cost, limit=24 << 20):
+def call(body, out_shape, in_specs, cost, limit=24 << 20, copies=0):
     flops, moved, exps = cost
     return pl.pallas_call(
         body,
         out_shape=out_shape,
         in_specs=in_specs,
         out_specs=jax.tree.map(lambda _: VMEM, out_shape),
+        scratch_shapes=[pltpu.SemaphoreType.DMA((copies,))] if copies else [],
         compiler_params=pltpu.CompilerParams(vmem_limit_bytes=limit),
         cost_estimate=pl.CostEstimate(
             flops=flops, bytes_accessed=moved, transcendentals=exps
@@ -51,25 +53,38 @@
     )
 
 
-def text_body(kt, vt, out):
+def text_body(kt, vt, out, sems):
     text = out.shape[0]
     width = kt.shape[2]
     _, _, sample, _ = place()
     rows = pl.ds(pl.multiple_of((1 - sample) * text, text), text)
-    out[:, :width] = kt[0, rows, :]
-    out[:, width:] = vt[0, rows, :]
-
-
-def pack_body(k, v, kt, vt, got, out):
+    copies = [
+        pltpu.make_async_copy(kt.at[0, rows, :], out.at[:, :width], sems.at[0]),
+        pltpu.make_async_copy(vt.at[0, rows, :], out.at[:, width:], sems.at[1]),
+    ]
+    for copy in copies:
+        copy.start()
+    for copy in copies:
+        copy.wait()
+
+
+def pack_body(k, v, kt, vt, got, out, sems):
     rows, width = k.shape[1:]
     text = got.shape[0]
     _, _, sample, _ = place()
     mine = pl.ds(pl.multiple_of(sample * text, text), text)
-    out[:rows, :width] = k[0]
-    out[:rows, width:] = v[0]
-    out[rows : rows + text, :width] = kt[0, mine, :]
-    out[rows : rows + text, width:] = vt[0, mine, :]
+    own = pl.ds(rows, text)
+    copies = [
+        pltpu.make_async_copy(k.at[0], out.at[:rows, :width], sems.at[0]),
+        pltpu.make_async_copy(v.at[0], out.at[:rows, width:], sems.at[1]),
+        pltpu.make_async_copy(kt.at[0, mine, :], out.at[own, :width], sems.at[2]),
+        pltpu.make_async_copy(vt.at[0, mine, :], out.at[own, width:], sems.at[3]),
+    ]
+    for copy in copies:
+        copy.start()
     out[rows + text :, :] = got[...]
+    for copy in copies:
+        copy.wait()
 
 
 def attend_body(kinds, first, last, row_count, *refs):
@@ -182,7 +197,15 @@
     )(*args)
 
 
-def merge_body(got, near, log, out):
+def merge_body(x_size, got, near, log, gates, out, gate_out):
+    blocks, _, gate_width = gates.shape
+    z_size = blocks // x_size
+    me = lax.axis_index("dp")
+    first = lax.axis_index("head") * (blocks // 2)
+    for j in range(blocks // 2):
+        by_x = lax.rem(lax.rem(me, x_size) - lax.rem(first + j, x_size) + x_size, x_size)
+        by_z = lax.rem(lax.div(me, x_size) - lax.div(first + j, x_size) + z_size, z_size)
+        gate_out[:, j * gate_width : (j + 1) * gate_width] = gates[by_z * x_size + by_x]
     rows, half = near.shape
     terms = [got[rows:, n * 256 : (n + 1) * 256].astype(F32) for n in range(3)]
     theirs = jnp.transpose(terms[0] + terms[1] + terms[2])
@@ -201,17 +224,9 @@
     out[...] = jnp.dot(mine[...], w_own[...], preferred_element_type=F32)
 
 
-def project_last_body(x_size, partial, theirs, w_got, gates, out):
+def project_last_body(partial, theirs, w_got, gate, out):
     total = partial[...] + jnp.dot(theirs[...], w_got[...], preferred_element_type=F32)
-    blocks, _, gate_width = gates.shape
-    z_size = blocks // x_size
-    me = lax.axis_index("dp")
-    first = lax.axis_index("head") * (blocks // 2)
-    for j in range(blocks // 2):
-        by_x = lax.rem(lax.rem(me, x_size) - lax.rem(first + j, x_size) + x_size, x_size)
-        by_z = lax.rem(lax.div(me, x_size) - lax.div(first + j, x_size) + z_size, z_size)
-        cols = slice(j * gate_width, (j + 1) * gate_width)
-        out[0, :, cols] = (total[:, cols] * gates[by_z * x_size + by_x]).astype(BF16)
+    out[0] = (total * gate[...]).astype(BF16)
 
 
 def gather_gates(gate, x_size, z_size):
@@ -240,11 +255,15 @@
         return jax.ShapeDtypeStruct(dims, BF16)
 
     t_send = call(
-        text_body, shape(text, 2 * width), [VMEM] * 2, (0, 8 * text * width, 0)
+        text_body, shape(text, 2 * width), [ANY] * 2, (0, 8 * text * width, 0), copies=2
     )(k_txt, v_txt)
     t_got = move(t_send, row_count, 0, -1)
     block = call(
-        pack_body, shape(rows + 2 * text, 2 * width), [VMEM] * 5, (0, 8 * rows * width, 0)
+        pack_body,
+        shape(rows + 2 * text, 2 * width),
+        [ANY] * 4 + [VMEM],
+        (0, 8 * rows * width, 0),
+        copies=4,
     )(k_img, v_img, k_txt, v_txt, t_got)
     q_got = move(q_img, row_count, 0, 2)
 
@@ -276,9 +295,12 @@
     gates = gather_gates(branch_gate, 4, lax.axis_size("dp") // 4)
 
     o_got = move(o_far, row_count, 0, 2)
-    mine = call(
-        merge_body, shape(rows, width), [VMEM] * 3, (0, 8 * rows * width, 0)
-    )(o_got, o_near, o_log)
+    mine, gate = call(
+        functools.partial(merge_body, 4),
+        (shape(rows, width), jax.ShapeDtypeStruct((1, out_width), F32)),
+        [VMEM] * 4,
+        (0, 8 * rows * width, 0),
+    )(o_got, o_near, o_log, gates)
     theirs = swap_cores(mine)
     partial = call(
         project_first_body,
@@ -287,11 +309,11 @@
         (2 * rows * width * out_width, 2 * width * out_width, 0),
     )(mine, w_own)
     return call(
-        functools.partial(project_last_body, 4),
+        project_last_body,
         shape(1, rows, out_width),
         [VMEM] * 4,
         (2 * rows * width * out_width, 2 * width * out_width, 0),
-    )(partial, theirs, w_got, gates)
+    )(partial, theirs, w_got, gate)
 
 
 def solution(mesh):

time: 125 us -> 134 us (1.072)
  the two profiles are of different devices: /device:TPU:1 before, /device:TPU:67 now
where the time goes in v2:
time: 134 us
  starting transfers between devices  70.4 us (53%)
  waiting for transfers between devices  41.7 us (31%)
  Pallas kernels  15 us (11%)
  local copies, waits for them, and re-layouts  6.2 us (5%)
    ppermute x11, starting transfers between devices, move(): return lax.ppermute(array, 'seq', pairs)  52.5 us
    ppermute x11, waiting for transfers between devices, move(): return lax.ppermute(array, 'seq', pairs)  39.6 us
    pallas_call x4, Pallas kernels, attend(): call(functools.partial(attend_body, kinds, state is None, last, row_count...  12.4 us
    ppermute x4, starting transfers between devices, along(): return lax.ppermute(array, 'dp', pairs)  10.7 us
    ppermute x2, starting transfers between devices, swap_cores(): return lax.ppermute(array, 'head', [(0, 1), (1, 0)])  7.21 us
    unnamed x18, local copies, waits for them, and re-layouts  3.43 us
    dynamic_slice x1, local copies, waits for them, and re-layouts, per_device(): lax.dynamic_slice_in_dim(w_out, (1 - core) * out_width, out_width, 1)  2.72 us
  transfers between devices with their start and end apart: 17, of which 7 were waited for; matrix products, arithmetic and copies ran while one was open for 2% of the time, Pallas kernels for 10%

profile of v2, /device:TPU:67, one launch (start us, length us, event | category | flops | bytes accessed | tf_op | source)
XLA Modules:
  0.0 133.7 jit_solution(9246928818635107517)
XLA Ops:
  0.0 0.7 copy-done.3
  0.7 0.7 copy-done.4
  1.5 13.4 %collective-permute-start.1 = (bf16[8,1536]{1,0:T(8,128)(2,1)S(1)}, bf16[8,1536]{1,0:T(8,128)(2,1)S(1)}, u32[]{:S(2)}, u32[]{:S(2)}) collective-permute-start(bf16[8,1536]{1,0:T(8,128)(2,1)S(1)} %shard_map.82), channel_id=1, source_target_pairs={{0,6},{2,0},{4,2},{6,4},{8,14},{10,8},{12,10},{14,12},{16,22},{18,... | collective-permute-start | bytes 73736 | tf_op jit(solution)/shard_map/ppermute | solution.py:34
  14.9 0.9 collective-permute-done.1.got
  15.8 1.0 copy-done.1
  16.8 1.0 copy-done.2
  17.7 0.1 shard_map.83.refs_3_
  17.9 3.2 %collective-permute-start.2 = (bf16[192,1536]{1,0:T(8,128)(2,1)S(1)}, bf16[192,1536]{1,0:T(8,128)(2,1)S(1)}, u32[]{:S(2)}, u32[]{:S(2)}) collective-permute-start(bf16[192,1536]{1,0:T(8,128)(2,1)S(1)} %shard_map.83.refs_3_), channel_id=1, source_target_pairs={{0,8},{2,10},{4,12},{6,14},{8,16},{10,18},{12,20},{14,22},{16,24},... | collective-permute-start | bytes 1769480 | tf_op jit(solution)/shard_map/ppermute | solution.py:34
  21.1 3.8 %collective-permute-start.6 = (bf16[192,1536]{1,0:T(8,128)(2,1)S(1)}, bf16[192,1536]{1,0:T(8,128)(2,1)S(1)}, u32[]{:S(2)}, u32[]{:S(2)}) collective-permute-start(bf16[192,1536]{1,0:T(8,128)(2,1)S(1)} %shard_map.83.refs_3_), channel_id=1, source_target_pairs={{0,56},{2,58},{4,60},{6,62},{8,0},{10,2},{12,4},{14,6},{16,8},{18,... | collective-permute-start | bytes 1769480 | tf_op jit(solution)/shard_map/ppermute | solution.py:34
  24.9 0.0 copy-start
  24.9 0.0 copy-start.6
  24.9 0.0 copy-start.5
  24.9 2.7 %constant_dynamic-slice_fusion = (bf16[768,1536]{1,0:T(8,128)(2,1)S(1)}, bf16[768,1536]{1,0:T(8,128)(2,1)S(1)}) fusion(bf16[768,3072]{1,0:T(8,128)(2,1)} %param.14, s32[]{:T(128)S(6)} %select_n.7, s32[]{:T(128)S(6)} %select_n.6), kind=kLoop, calls=%fused_computation.7 | loop fusion | bytes 9437192 | tf_op jit(solution)/shard_map/dynamic_slice | solution.py:292
  27.7 3.7 %collective-permute-start.16 = (bf16[768,1536]{1,0:T(8,128)(2,1)S(1)}, bf16[768,1536]{1,0:T(8,128)(2,1)S(1)}, u32[]{:S(2)}, u32[]{:S(2)}) collective-permute-start(bf16[768,1536]{1,0:T(8,128)(2,1)S(1)} %get-tuple-element.27), channel_id=1, source_target_pairs={{0,1},{1,0},{2,3},{3,2},{4,5},{5,4},{6,7},{7,6},{8,9},{9,8},{10,11... | collective-permute-start | bytes 7077896 | tf_op jit(solution)/shard_map/ppermute | solution.py:38
  31.4 3.7 %collective-permute-done.2.refs_4_ = bf16[192,1536]{1,0:T(8,128)(2,1)S(1)} collective-permute-done((bf16[192,1536]{1,0:T(8,128)(2,1)S(1)}, bf16[192,1536]{1,0:T(8,128)(2,1)S(1)}, u32[]{:S(2)}, u32[]{:S(2)}) %collective-permute-start.2) | collective-permute-done | bytes 589856 | tf_op jit(solution)/shard_map/ppermute | solution.py:34
  35.1 1.9 %collective-permute-start.3 = (bf16[192,1536]{1,0:T(8,128)(2,1)S(1)}, bf16[192,1536]{1,0:T(8,128)(2,1)S(1)}, u32[]{:S(2)}, u32[]{:S(2)}) collective-permute-start(bf16[192,1536]{1,0:T(8,128)(2,1)S(1)} %collective-permute-done.2.refs_4_), channel_id=1, source_target_pairs={{0,8},{2,10},{4,12},{6,14},{8,16},{10,18},{12,20},{14,22},{16,24},... | collective-permute-start | bytes 1769480 | tf_op jit(solution)/shard_map/ppermute | solution.py:34
  37.0 0.0 collective-permute-done.6.refs_5_
  37.0 4.6 %collective-permute-start.7 = (bf16[192,1536]{1,0:T(8,128)(2,1)S(1)}, bf16[192,1536]{1,0:T(8,128)(2,1)S(1)}, u32[]{:S(2)}, u32[]{:S(2)}) collective-permute-start(bf16[192,1536]{1,0:T(8,128)(2,1)S(1)} %collective-permute-done.6.refs_5_), channel_id=1, source_target_pairs={{0,56},{2,58},{4,60},{6,62},{8,0},{10,2},{12,4},{14,6},{16,8},{18,... | collective-permute-start | bytes 1769480 | tf_op jit(solution)/shard_map/ppermute | solution.py:34
  41.6 9.4 %collective-permute-done.3.refs_3_ = bf16[192,1536]{1,0:T(8,128)(2,1)S(1)} collective-permute-done((bf16[192,1536]{1,0:T(8,128)(2,1)S(1)}, bf16[192,1536]{1,0:T(8,128)(2,1)S(1)}, u32[]{:S(2)}, u32[]{:S(2)}) %collective-permute-start.3) | collective-permute-done | bytes 589856 | tf_op jit(solution)/shard_map/ppermute | solution.py:34
  51.0 1.9 %collective-permute-start.4 = (bf16[192,1536]{1,0:T(8,128)(2,1)S(1)}, bf16[192,1536]{1,0:T(8,128)(2,1)S(1)}, u32[]{:S(2)}, u32[]{:S(2)}) collective-permute-start(bf16[192,1536]{1,0:T(8,128)(2,1)S(1)} %collective-permute-done.3.refs_3_), channel_id=1, source_target_pairs={{0,8},{2,10},{4,12},{6,14},{8,16},{10,18},{12,20},{14,22},{16,24},... | collective-permute-start | bytes 1769480 | tf_op jit(solution)/shard_map/ppermute | solution.py:34
  52.9 0.0 collective-permute-done.7.refs_4_
  52.9 4.6 %collective-permute-start.8 = (bf16[192,1536]{1,0:T(8,128)(2,1)S(1)}, bf16[192,1536]{1,0:T(8,128)(2,1)S(1)}, u32[]{:S(2)}, u32[]{:S(2)}) collective-permute-start(bf16[192,1536]{1,0:T(8,128)(2,1)S(1)} %collective-permute-done.7.refs_4_), channel_id=1, source_target_pairs={{0,56},{2,58},{4,60},{6,62},{8,0},{10,2},{12,4},{14,6},{16,8},{18,... | collective-permute-start | bytes 1769480 | tf_op jit(solution)/shard_map/ppermute | solution.py:34
  57.5 6.8 %collective-permute-start = (bf16[1,176,768]{2,1,0:T(8,128)(2,1)S(1)}, bf16[1,176,768]{2,1,0:T(8,128)(2,1)S(1)}, u32[]{:S(2)}, u32[]{:S(2)}) collective-permute-start(bf16[1,176,768]{2,1,0:T(8,128)(2,1)S(1)} %copy-done), channel_id=1, source_target_pairs={{0,4},{2,6},{4,0},{6,2},{8,12},{10,14},{12,8},{14,10},{16,20},{18,... | collective-permute-start | bytes 811016 | tf_op jit(solution)/shard_map/ppermute | solution.py:34
  64.4 3.1 %collective-permute-start.11 = (f32[1,1,256]{2,1,0:T(1,128)S(1)}, f32[1,1,256]{2,1,0:T(1,128)S(1)}, u32[]{:S(2)}, u32[]{:S(2)}) collective-permute-start(f32[1,1,256]{2,1,0:T(1,128)S(1)} %bitcast.1), channel_id=1, source_target_pairs={{0,64},{64,128},{128,192},{192,0},{256,320},{320,384},{384,448},{4... | collective-permute-start | bytes 3080 | tf_op jit(solution)/shard_map/ppermute | solution.py:239
  67.5 1.5 %collective-permute-done.11 = f32[1,1,256]{2,1,0:T(1,128)S(1)} collective-permute-done((f32[1,1,256]{2,1,0:T(1,128)S(1)}, f32[1,1,256]{2,1,0:T(1,128)S(1)}, u32[]{:S(2)}, u32[]{:S(2)}) %collective-permute-start.11) | collective-permute-done | bytes 1056 | tf_op jit(solution)/shard_map/ppermute | solution.py:239
  69.0 3.7 %collective-permute-start.12 = (f32[2,1,256]{2,1,0:T(1,128)S(1)}, f32[2,1,256]{2,1,0:T(1,128)S(1)}, u32[]{:S(2)}, u32[]{:S(2)}) collective-permute-start(f32[2,1,256]{2,1,0:T(1,128)S(1)} %pad_maximum_fusion.1), channel_id=1, source_target_pairs={{0,128},{64,192},{128,0},{192,64},{256,384},{320,448},{384,256},{4... | collective-permute-start | bytes 6152 | tf_op jit(solution)/shard_map/ppermute | solution.py:239
  72.7 0.0 collective-permute-done.4.refs_3_
  72.8 1.9 %collective-permute-start.5 = (bf16[96,1536]{1,0:T(8,128)(2,1)S(1)}, bf16[96,1536]{1,0:T(8,128)(2,1)S(1)}, u32[]{:S(2)}, u32[]{:S(2)}) collective-permute-start(bf16[96,1536]{1,0:T(8,128)(2,1)S(1)} %slice.8), channel_id=1, source_target_pairs={{0,8},{2,10},{4,12},{6,14},{8,16},{10,18},{12,20},{14,22},{16,24},... | collective-permute-start | bytes 884744 | tf_op jit(solution)/shard_map/ppermute | solution.py:34
  74.7 0.0 collective-permute-done.8.refs_4_
  74.7 4.6 %collective-permute-start.9 = (bf16[96,1536]{1,0:T(8,128)(2,1)S(1)}, bf16[96,1536]{1,0:T(8,128)(2,1)S(1)}, u32[]{:S(2)}, u32[]{:S(2)}) collective-permute-start(bf16[96,1536]{1,0:T(8,128)(2,1)S(1)} %slice.9), channel_id=1, source_target_pairs={{0,56},{2,58},{4,60},{6,62},{8,0},{10,2},{12,4},{14,6},{16,8},{18,... | collective-permute-start | bytes 884744 | tf_op jit(solution)/shard_map/ppermute | solution.py:34
  79.3 0.0 collective-permute-done.12
  79.4 1.9 %collective-permute-start.13 = (f32[4,1,256]{2,1,0:T(1,128)S(1)}, f32[4,1,256]{2,1,0:T(1,128)S(1)}, u32[]{:S(2)}, u32[]{:S(2)}) collective-permute-start(f32[4,1,256]{2,1,0:T(1,128)S(1)} %pad_maximum_fusion), channel_id=1, source_target_pairs={{0,256},{64,320},{128,384},{192,448},{256,512},{320,576},{384,640}... | collective-permute-start | bytes 12296 | tf_op jit(solution)/shard_map/ppermute | solution.py:239
  81.3 3.7 %collective-permute-done.refs_2_ = bf16[1,176,768]{2,1,0:T(8,128)(2,1)S(1)} collective-permute-done((bf16[1,176,768]{2,1,0:T(8,128)(2,1)S(1)}, bf16[1,176,768]{2,1,0:T(8,128)(2,1)S(1)}, u32[]{:S(2)}, u32[]{:S(2)}) %collective-permute-start) | collective-permute-done | bytes 270368 | tf_op jit(solution)/shard_map/ppermute | solution.py:34
  85.0 1.9 %collective-permute-start.14 = (f32[4,1,256]{2,1,0:T(1,128)S(1)}, f32[4,1,256]{2,1,0:T(1,128)S(1)}, u32[]{:S(2)}, u32[]{:S(2)}) collective-permute-start(f32[4,1,256]{2,1,0:T(1,128)S(1)} %pad_maximum_fusion), channel_id=1, source_target_pairs={{0,512},{64,576},{128,640},{192,704},{256,0},{320,64},{384,128},{4... | collective-permute-start | bytes 12296 | tf_op jit(solution)/shard_map/ppermute | solution.py:239
  86.9 3.8 %shard_map.84 = (f32[768,384]{1,0:T(8,128)S(1)}, f32[16,384]{1,0:T(8,128)S(1)}) custom-call(s32[1,2]{1,0:T(1,128)S(1)} %copy-done.5, bf16[1,176,768]{2,1,0:T(8,128)(2,1)S(1)} %copy-done, bf16[1,176,768]{2,1,0:T(8,128)(2,1)S(1)} %collective-permute-done.refs_2_, bf16[192,1536]{1,0:T(8,128)(2,1)S(1)} %shard_map.83.refs_3_, ...), custom_call_target="tpu_custom_call" | custom-call | flops 679477248 | bytes 2310148 | tf_op jit(solution)/shard_map/pallas_call | solution.py:192
  90.7 3.1 %shard_map.85 = (f32[768,384]{1,0:T(8,128)S(1)}, f32[16,384]{1,0:T(8,128)S(1)}) custom-call(s32[1,2]{1,0:T(1,128)S(1)} %copy-done.5, bf16[1,176,768]{2,1,0:T(8,128)(2,1)S(1)} %copy-done, bf16[1,176,768]{2,1,0:T(8,128)(2,1)S(1)} %collective-permute-done.refs_2_, bf16[192,1536]{1,0:T(8,128)(2,1)S(1)} %collective-permute-done.3.refs_3_, ...), custom_call_target="tpu_custom_call" | custom-call | flops 452984832 | bytes 2322436 | tf_op jit(solution)/shard_map/pallas_call | solution.py:192
  93.8 3.1 %shard_map.86 = (f32[768,384]{1,0:T(8,128)S(1)}, f32[16,384]{1,0:T(8,128)S(1)}) custom-call(s32[1,2]{1,0:T(1,128)S(1)} %copy-done.5, bf16[1,176,768]{2,1,0:T(8,128)(2,1)S(1)} %copy-done, bf16[1,176,768]{2,1,0:T(8,128)(2,1)S(1)} %collective-permute-done.refs_2_, bf16[192,1536]{1,0:T(8,128)(2,1)S(1)} %collective-permute-done.4.refs_3_, ...), custom_call_target="tpu_custom_call" | custom-call | flops 452984832 | bytes 2322436 | tf_op jit(solution)/shard_map/pallas_call | solution.py:192
  96.9 0.0 collective-permute-done.5.refs_3_
  96.9 2.5 %shard_map.87 = (bf16[184,768]{1,0:T(8,128)(2,1)S(1)}, f32[176,768]{1,0:T(8,128)S(1)}, f32[8,384]{1,0:T(8,128)S(1)}) custom-call(s32[1,2]{1,0:T(1,128)S(1)} %copy-done.5, bf16[1,176,768]{2,1,0:T(8,128)(2,1)S(1)} %copy-done, bf16[1,176,768]{2,1,0:T(8,128)(2,1)S(1)} %collective-permute-done.refs_2_, bf16[96,1536]{1,0:T(8,128)(2,1)S(1)} %collective-permute-done.5.refs_3_, ...), custom_call_target="tpu_custom_call" | custom-call | flops 226492416 | bytes 1732612 | tf_op jit(solution)/shard_map/pallas_call | solution.py:192
  99.4 5.9 %collective-permute-start.10 = (bf16[184,768]{1,0:T(8,128)(2,1)S(1)}, bf16[184,768]{1,0:T(8,128)(2,1)S(1)}, u32[]{:S(2)}, u32[]{:S(2)}) collective-permute-start(bf16[184,768]{1,0:T(8,128)(2,1)S(1)} %get-tuple-element.22), channel_id=1, source_target_pairs={{0,4},{2,6},{4,0},{6,2},{8,12},{10,14},{12,8},{14,10},{16,20},{18,... | collective-permute-start | bytes 847880 | tf_op jit(solution)/shard_map/ppermute | solution.py:34
  105.3 0.0 collective-permute-done.14
  105.3 21.8 %collective-permute-done.10.got = bf16[184,768]{1,0:T(8,128)(2,1)S(1)} collective-permute-done((bf16[184,768]{1,0:T(8,128)(2,1)S(1)}, bf16[184,768]{1,0:T(8,128)(2,1)S(1)}, u32[]{:S(2)}, u32[]{:S(2)}) %collective-permute-start.10) | collective-permute-done | bytes 282656 | tf_op jit(solution)/shard_map/ppermute | solution.py:34
  127.2 0.5 shard_map.88
  127.6 3.5 %collective-permute-start.15 = (bf16[176,768]{1,0:T(8,128)(2,1)S(1)}, bf16[176,768]{1,0:T(8,128)(2,1)S(1)}, u32[]{:S(2)}, u32[]{:S(2)}) collective-permute-start(bf16[176,768]{1,0:T(8,128)(2,1)S(1)} %get-tuple-element.25.mine), channel_id=1, source_target_pairs={{0,1},{1,0},{2,3},{3,2},{4,5},{5,4},{6,7},{7,6},{8,9},{9,8},{10,11... | collective-permute-start | bytes 811016 | tf_op jit(solution)/shard_map/ppermute | solution.py:38
  131.1 0.6 shard_map.89.partial
  131.7 0.0 collective-permute-done.16.w_got
  131.7 0.6 collective-permute-done.15.theirs
  132.3 1.4 %shard_map.90 = bf16[1,176,1536]{2,1,0:T(8,128)(2,1)} custom-call(f32[176,1536]{1,0:T(8,128)S(1)} %shard_map.89.partial, bf16[176,768]{1,0:T(8,128)(2,1)S(1)} %collective-permute-done.15.theirs, bf16[768,1536]{1,0:T(8,128)(2,1)S(1)} %collective-permute-done.16.w_got, f32[1,1536]{1,0:T(1,128)S(1)} %get-tuple-element.26.gate), custom_call_target="tpu_custom_call" | custom-call | flops 415236096 | bytes 2359296 | tf_op jit(solution)/shard_map/pallas_call | solution.py:311
  (19 shorter events, 0.1 us)
Async XLA Ops:
  0.0 0.7 copy-start.3
  0.7 0.7 copy-start.4
  1.5 14.3 %collective-permute-start.1 = (bf16[8,1536]{1,0:T(8,128)(2,1)S(1)}, bf16[8,1536]{1,0:T(8,128)(2,1)S(1)}, u32[]{:S(2)}, u32[]{:S(2)}) collective-permute-start(bf16[8,1536]{1,0:T(8,128)(2,1)S(1)} %shard_map.82), channel_id=1, source_target_pairs={{0,6},{2,0},{4,2},{6,4},{8,14},{10,8},{12,10},{14,12},{16,22},{18,... | collective-permute-start | bytes 73736 | tf_op jit(solution)/shard_map/ppermute | solution.py:34
  15.8 1.0 copy-start.1
  16.8 1.0 copy-start.2
  17.9 17.3 %collective-permute-start.2 = (bf16[192,1536]{1,0:T(8,128)(2,1)S(1)}, bf16[192,1536]{1,0:T(8,128)(2,1)S(1)}, u32[]{:S(2)}, u32[]{:S(2)}) collective-permute-start(bf16[192,1536]{1,0:T(8,128)(2,1)S(1)} %shard_map.83.refs_3_), channel_id=1, source_target_pairs={{0,8},{2,10},{4,12},{6,14},{8,16},{10,18},{12,20},{14,22},{16,24},... | collective-permute-start | bytes 1769480 | tf_op jit(solution)/shard_map/ppermute | solution.py:34
  21.1 16.0 %collective-permute-start.6 = (bf16[192,1536]{1,0:T(8,128)(2,1)S(1)}, bf16[192,1536]{1,0:T(8,128)(2,1)S(1)}, u32[]{:S(2)}, u32[]{:S(2)}) collective-permute-start(bf16[192,1536]{1,0:T(8,128)(2,1)S(1)} %shard_map.83.refs_3_), channel_id=1, source_target_pairs={{0,56},{2,58},{4,60},{6,62},{8,0},{10,2},{12,4},{14,6},{16,8},{18,... | collective-permute-start | bytes 1769480 | tf_op jit(solution)/shard_map/ppermute | solution.py:34
  24.9 32.6 %copy-start = (bf16[1,176,768]{2,1,0:T(8,128)(2,1)S(1)}, bf16[1,176,768]{2,1,0:T(8,128)(2,1)}, u32[]{:S(2)}) copy-start(bf16[1,176,768]{2,1,0:T(8,128)(2,1)} %refs_1_.7) | copy-start | bytes 811012
  24.9 39.4 %copy-start.6 = (f32[256]{0:T(256)S(1)}, f32[256]{0:T(256)}, u32[]{:S(2)}) copy-start(f32[256]{0:T(256)} %param.15) | copy-start | bytes 3076
  24.9 62.0 %copy-start.5 = (s32[1,2]{1,0:T(1,128)S(1)}, s32[1,2]{1,0:T(1,128)}, u32[]{:S(2)}) copy-start(s32[1,2]{1,0:T(1,128)} %refs_0_.7) | copy-start | bytes 28
  27.7 104.1 %collective-permute-start.16 = (bf16[768,1536]{1,0:T(8,128)(2,1)S(1)}, bf16[768,1536]{1,0:T(8,128)(2,1)S(1)}, u32[]{:S(2)}, u32[]{:S(2)}) collective-permute-start(bf16[768,1536]{1,0:T(8,128)(2,1)S(1)} %get-tuple-element.27), channel_id=1, source_target_pairs={{0,1},{1,0},{2,3},{3,2},{4,5},{5,4},{6,7},{7,6},{8,9},{9,8},{10,11... | collective-permute-start | bytes 7077896 | tf_op jit(solution)/shard_map/ppermute | solution.py:38
  35.1 15.9 %collective-permute-start.3 = (bf16[192,1536]{1,0:T(8,128)(2,1)S(1)}, bf16[192,1536]{1,0:T(8,128)(2,1)S(1)}, u32[]{:S(2)}, u32[]{:S(2)}) collective-permute-start(bf16[192,1536]{1,0:T(8,128)(2,1)S(1)} %collective-permute-done.2.refs_4_), channel_id=1, source_target_pairs={{0,8},{2,10},{4,12},{6,14},{8,16},{10,18},{12,20},{14,22},{16,24},... | collective-permute-start | bytes 1769480 | tf_op jit(solution)/shard_map/ppermute | solution.py:34
  37.0 15.9 %collective-permute-start.7 = (bf16[192,1536]{1,0:T(8,128)(2,1)S(1)}, bf16[192,1536]{1,0:T(8,128)(2,1)S(1)}, u32[]{:S(2)}, u32[]{:S(2)}) collective-permute-start(bf16[192,1536]{1,0:T(8,128)(2,1)S(1)} %collective-permute-done.6.refs_5_), channel_id=1, source_target_pairs={{0,56},{2,58},{4,60},{6,62},{8,0},{10,2},{12,4},{14,6},{16,8},{18,... | collective-permute-start | bytes 1769480 | tf_op jit(solution)/shard_map/ppermute | solution.py:34
  51.0 21.7 %collective-permute-start.4 = (bf16[192,1536]{1,0:T(8,128)(2,1)S(1)}, bf16[192,1536]{1,0:T(8,128)(2,1)S(1)}, u32[]{:S(2)}, u32[]{:S(2)}) collective-permute-start(bf16[192,1536]{1,0:T(8,128)(2,1)S(1)} %collective-permute-done.3.refs_3_), channel_id=1, source_target_pairs={{0,8},{2,10},{4,12},{6,14},{8,16},{10,18},{12,20},{14,22},{16,24},... | collective-permute-start | bytes 1769480 | tf_op jit(solution)/shard_map/ppermute | solution.py:34
  52.9 21.8 %collective-permute-start.8 = (bf16[192,1536]{1,0:T(8,128)(2,1)S(1)}, bf16[192,1536]{1,0:T(8,128)(2,1)S(1)}, u32[]{:S(2)}, u32[]{:S(2)}) collective-permute-start(bf16[192,1536]{1,0:T(8,128)(2,1)S(1)} %collective-permute-done.7.refs_4_), channel_id=1, source_target_pairs={{0,56},{2,58},{4,60},{6,62},{8,0},{10,2},{12,4},{14,6},{16,8},{18,... | collective-permute-start | bytes 1769480 | tf_op jit(solution)/shard_map/ppermute | solution.py:34
  57.5 27.5 %collective-permute-start = (bf16[1,176,768]{2,1,0:T(8,128)(2,1)S(1)}, bf16[1,176,768]{2,1,0:T(8,128)(2,1)S(1)}, u32[]{:S(2)}, u32[]{:S(2)}) collective-permute-start(bf16[1,176,768]{2,1,0:T(8,128)(2,1)S(1)} %copy-done), channel_id=1, source_target_pairs={{0,4},{2,6},{4,0},{6,2},{8,12},{10,14},{12,8},{14,10},{16,20},{18,... | collective-permute-start | bytes 811016 | tf_op jit(solution)/shard_map/ppermute | solution.py:34
  64.4 4.6 %collective-permute-start.11 = (f32[1,1,256]{2,1,0:T(1,128)S(1)}, f32[1,1,256]{2,1,0:T(1,128)S(1)}, u32[]{:S(2)}, u32[]{:S(2)}) collective-permute-start(f32[1,1,256]{2,1,0:T(1,128)S(1)} %bitcast.1), channel_id=1, source_target_pairs={{0,64},{64,128},{128,192},{192,0},{256,320},{320,384},{384,448},{4... | collective-permute-start | bytes 3080 | tf_op jit(solution)/shard_map/ppermute | solution.py:239
  69.0 10.4 %collective-permute-start.12 = (f32[2,1,256]{2,1,0:T(1,128)S(1)}, f32[2,1,256]{2,1,0:T(1,128)S(1)}, u32[]{:S(2)}, u32[]{:S(2)}) collective-permute-start(f32[2,1,256]{2,1,0:T(1,128)S(1)} %pad_maximum_fusion.1), channel_id=1, source_target_pairs={{0,128},{64,192},{128,0},{192,64},{256,384},{320,448},{384,256},{4... | collective-permute-start | bytes 6152 | tf_op jit(solution)/shard_map/ppermute | solution.py:239
  72.8 24.1 %collective-permute-start.5 = (bf16[96,1536]{1,0:T(8,128)(2,1)S(1)}, bf16[96,1536]{1,0:T(8,128)(2,1)S(1)}, u32[]{:S(2)}, u32[]{:S(2)}) collective-permute-start(bf16[96,1536]{1,0:T(8,128)(2,1)S(1)} %slice.8), channel_id=1, source_target_pairs={{0,8},{2,10},{4,12},{6,14},{8,16},{10,18},{12,20},{14,22},{16,24},... | collective-permute-start | bytes 884744 | tf_op jit(solution)/shard_map/ppermute | solution.py:34
  74.7 22.2 %collective-permute-start.9 = (bf16[96,1536]{1,0:T(8,128)(2,1)S(1)}, bf16[96,1536]{1,0:T(8,128)(2,1)S(1)}, u32[]{:S(2)}, u32[]{:S(2)}) collective-permute-start(bf16[96,1536]{1,0:T(8,128)(2,1)S(1)} %slice.9), channel_id=1, source_target_pairs={{0,56},{2,58},{4,60},{6,62},{8,0},{10,2},{12,4},{14,6},{16,8},{18,... | collective-permute-start | bytes 884744 | tf_op jit(solution)/shard_map/ppermute | solution.py:34
  79.4 25.9 %collective-permute-start.13 = (f32[4,1,256]{2,1,0:T(1,128)S(1)}, f32[4,1,256]{2,1,0:T(1,128)S(1)}, u32[]{:S(2)}, u32[]{:S(2)}) collective-permute-start(f32[4,1,256]{2,1,0:T(1,128)S(1)} %pad_maximum_fusion), channel_id=1, source_target_pairs={{0,256},{64,320},{128,384},{192,448},{256,512},{320,576},{384,640}... | collective-permute-start | bytes 12296 | tf_op jit(solution)/shard_map/ppermute | solution.py:239
  85.0 20.3 %collective-permute-start.14 = (f32[4,1,256]{2,1,0:T(1,128)S(1)}, f32[4,1,256]{2,1,0:T(1,128)S(1)}, u32[]{:S(2)}, u32[]{:S(2)}) collective-permute-start(f32[4,1,256]{2,1,0:T(1,128)S(1)} %pad_maximum_fusion), channel_id=1, source_target_pairs={{0,512},{64,576},{128,640},{192,704},{256,0},{320,64},{384,128},{4... | collective-permute-start | bytes 12296 | tf_op jit(solution)/shard_map/ppermute | solution.py:239
  99.4 27.8 %collective-permute-start.10 = (bf16[184,768]{1,0:T(8,128)(2,1)S(1)}, bf16[184,768]{1,0:T(8,128)(2,1)S(1)}, u32[]{:S(2)}, u32[]{:S(2)}) collective-permute-start(bf16[184,768]{1,0:T(8,128)(2,1)S(1)} %get-tuple-element.22), channel_id=1, source_target_pairs={{0,4},{2,6},{4,0},{6,2},{8,12},{10,14},{12,8},{14,10},{16,20},{18,... | collective-permute-start | bytes 847880 | tf_op jit(solution)/shard_map/ppermute | solution.py:34
  127.6 4.6 %collective-permute-start.15 = (bf16[176,768]{1,0:T(8,128)(2,1)S(1)}, bf16[176,768]{1,0:T(8,128)(2,1)S(1)}, u32[]{:S(2)}, u32[]{:S(2)}) collective-permute-start(bf16[176,768]{1,0:T(8,128)(2,1)S(1)} %get-tuple-element.25.mine), channel_id=1, source_target_pairs={{0,1},{1,0},{2,3},{3,2},{4,5},{5,4},{6,7},{7,6},{8,9},{9,8},{10,11... | collective-permute-start | bytes 811016 | tf_op jit(solution)/shard_map/ppermute | solution.py:38

commit v3 on v2

--- a/solution.py
+++ b/solution.py
@@ -15,7 +15,7 @@
 F32 = jnp.float32
 VMEM = pl.BlockSpec(memory_space=pltpu.VMEM)
 SMEM = pl.BlockSpec(memory_space=pltpu.SMEM)
-ANY = pl.BlockSpec(memory_space=pl.ANY)
+HBM = pl.BlockSpec(memory_space=pltpu.HBM)
 
 
 def place():
@@ -38,7 +38,7 @@
     return lax.ppermute(array, "head", [(0, 1), (1, 0)])
 
 
-def call(body, out_shape, in_specs, cost, limit=24 << 20, copies=0):
+def call(body, out_shape, in_specs, cost, limit=12 << 20, copies=0):
     flops, moved, exps = cost
     return pl.pallas_call(
         body,
@@ -205,7 +205,7 @@
     for j in range(blocks // 2):
         by_x = lax.rem(lax.rem(me, x_size) - lax.rem(first + j, x_size) + x_size, x_size)
         by_z = lax.rem(lax.div(me, x_size) - lax.div(first + j, x_size) + z_size, z_size)
-        gate_out[:, j * gate_width : (j + 1) * gate_width] = gates[by_z * x_size + by_x]
+        gate_out[:, j * gate_width : (j + 1) * gate_width] = gates[by_x * z_size + by_z]
     rows, half = near.shape
     terms = [got[rows:, n * 256 : (n + 1) * 256].astype(F32) for n in range(3)]
     theirs = jnp.transpose(terms[0] + terms[1] + terms[2])
@@ -238,30 +238,34 @@
         ]
         return lax.ppermute(array, "dp", pairs)
 
-    held = gate.reshape(1, 1, gate.shape[0])
+    own = gate.reshape(1, 1, gate.shape[0])
+    held = jnp.concatenate([own] + [along(own, i, 0) for i in range(1, z_size)], axis=0)
     step = 1
     while step < x_size:
         held = jnp.concatenate([held, along(held, 0, step)], axis=0)
         step *= 2
-    return jnp.concatenate([held] + [along(held, i, 0) for i in range(1, z_size)], axis=0)
+    return held
 
 
 def per_device(q_img, k_img, v_img, k_txt, v_txt, text_length, w_out, branch_gate):
     row_count = lax.axis_size("seq") // PLANES
     rows, width = q_img.shape[1:]
     text = k_txt.shape[1] // 2
+    k_img, v_img, k_txt, v_txt = (
+        pltpu.with_memory_space_constraint(x, pltpu.HBM) for x in (k_img, v_img, k_txt, v_txt)
+    )
 
     def shape(*dims):
         return jax.ShapeDtypeStruct(dims, BF16)
 
     t_send = call(
-        text_body, shape(text, 2 * width), [ANY] * 2, (0, 8 * text * width, 0), copies=2
+        text_body, shape(text, 2 * width), [HBM] * 2, (0, 8 * text * width, 0), copies=2
     )(k_txt, v_txt)
     t_got = move(t_send, row_count, 0, -1)
     block = call(
         pack_body,
         shape(rows + 2 * text, 2 * width),
-        [ANY] * 4 + [VMEM],
+        [HBM] * 4 + [VMEM],
         (0, 8 * rows * width, 0),
         copies=4,
     )(k_img, v_img, k_txt, v_txt, t_got)
@@ -271,7 +275,7 @@
     for _ in range(1, 4):
         up.append(move(up[-1], row_count, 1, 0))
         down.append(move(down[-1], row_count, -1, 0))
-    cut = (rows + 2 * text) // 2
+    cut = (rows + 2 * text) * 3 // 4
     up.append(move(up[3][:cut], row_count, 1, 0))
     down.append(move(down[3][cut:], row_count, -1, 0))
 

time: 134 us -> 132 us (0.985)
  the two profiles are of different devices: /device:TPU:67 before, /device:TPU:65 now
where the time goes in v3:
time: 132 us; the launch traced here: 131 us
  starting transfers between devices  71.5 us (54%)
  waiting for transfers between devices  39.4 us (30%)
  Pallas kernels  16.7 us (13%)
  local copies, waits for them, and re-layouts  2.78 us (2%)
    ppermute x11, starting transfers between devices, move(): return lax.ppermute(array, 'seq', pairs)  52.4 us
    ppermute x11, waiting for transfers between devices, move(): return lax.ppermute(array, 'seq', pairs)  37.3 us
    ppermute x4, starting transfers between devices, along(): return lax.ppermute(array, 'dp', pairs)  13.1 us
    pallas_call x4, Pallas kernels, attend(): call(functools.partial(attend_body, kinds, state is None, last, row_count...  12.4 us
    ppermute x2, starting transfers between devices, swap_cores(): return lax.ppermute(array, 'head', [(0, 1), (1, 0)])  6.11 us
    dynamic_slice x1, local copies, waits for them, and re-layouts, per_device(): lax.dynamic_slice_in_dim(w_out, (1 - core) * out_width, out_width, 1)  2.69 us
  transfers between devices with their start and end apart: 17, of which 8 were waited for; matrix products, arithmetic and copies ran while one was open for 2% of the time, Pallas kernels for 10%

profile of v3, /device:TPU:65, one launch (start us, length us, event | category | flops | bytes accessed | tf_op | source)
XLA Modules:
  0.0 130.8 jit_solution(15141604744801791515)
XLA Ops:
  0.0 0.7 shard_map.82
  0.7 13.4 %collective-permute-start.1 = (bf16[8,1536]{1,0:T(8,128)(2,1)S(1)}, bf16[8,1536]{1,0:T(8,128)(2,1)S(1)}, u32[]{:S(2)}, u32[]{:S(2)}) collective-permute-start(bf16[8,1536]{1,0:T(8,128)(2,1)S(1)} %shard_map.82), channel_id=1, source_target_pairs={{0,6},{2,0},{4,2},{6,4},{8,14},{10,8},{12,10},{14,12},{16,22},{18,... | collective-permute-start | bytes 73736 | tf_op jit(solution)/shard_map/ppermute | solution.py:34
  14.1 0.9 collective-permute-done.1.got
  15.1 1.1 shard_map.83.refs_3_
  16.1 3.2 %collective-permute-start.2 = (bf16[192,1536]{1,0:T(8,128)(2,1)S(1)}, bf16[192,1536]{1,0:T(8,128)(2,1)S(1)}, u32[]{:S(2)}, u32[]{:S(2)}) collective-permute-start(bf16[192,1536]{1,0:T(8,128)(2,1)S(1)} %shard_map.83.refs_3_), channel_id=1, source_target_pairs={{0,8},{2,10},{4,12},{6,14},{8,16},{10,18},{12,20},{14,22},{16,24},... | collective-permute-start | bytes 1769480 | tf_op jit(solution)/shard_map/ppermute | solution.py:34
  19.4 0.0 copy-start.2
  19.4 0.0 copy-start
  19.4 0.0 copy-start.1
  19.4 3.9 %collective-permute-start.6 = (bf16[192,1536]{1,0:T(8,128)(2,1)S(1)}, bf16[192,1536]{1,0:T(8,128)(2,1)S(1)}, u32[]{:S(2)}, u32[]{:S(2)}) collective-permute-start(bf16[192,1536]{1,0:T(8,128)(2,1)S(1)} %shard_map.83.refs_3_), channel_id=1, source_target_pairs={{0,56},{2,58},{4,60},{6,62},{8,0},{10,2},{12,4},{14,6},{16,8},{18,... | collective-permute-start | bytes 1769480 | tf_op jit(solution)/shard_map/ppermute | solution.py:34
  23.4 2.7 %constant_dynamic-slice_fusion = (bf16[768,1536]{1,0:T(8,128)(2,1)S(1)}, bf16[768,1536]{1,0:T(8,128)(2,1)S(1)}) fusion(bf16[768,3072]{1,0:T(8,128)(2,1)} %param.14, s32[]{:T(128)S(6)} %select_n.7, s32[]{:T(128)S(6)} %select_n.6), kind=kLoop, calls=%fused_computation.7 | loop fusion | bytes 9437192 | tf_op jit(solution)/shard_map/dynamic_slice | solution.py:296
  26.0 3.7 %collective-permute-start.16 = (bf16[768,1536]{1,0:T(8,128)(2,1)S(1)}, bf16[768,1536]{1,0:T(8,128)(2,1)S(1)}, u32[]{:S(2)}, u32[]{:S(2)}) collective-permute-start(bf16[768,1536]{1,0:T(8,128)(2,1)S(1)} %get-tuple-element.27), channel_id=1, source_target_pairs={{0,1},{1,0},{2,3},{3,2},{4,5},{5,4},{6,7},{7,6},{8,9},{9,8},{10,11... | collective-permute-start | bytes 7077896 | tf_op jit(solution)/shard_map/ppermute | solution.py:38
  29.8 3.6 %collective-permute-done.2.refs_4_ = bf16[192,1536]{1,0:T(8,128)(2,1)S(1)} collective-permute-done((bf16[192,1536]{1,0:T(8,128)(2,1)S(1)}, bf16[192,1536]{1,0:T(8,128)(2,1)S(1)}, u32[]{:S(2)}, u32[]{:S(2)}) %collective-permute-start.2) | collective-permute-done | bytes 589856 | tf_op jit(solution)/shard_map/ppermute | solution.py:34
  33.4 1.9 %collective-permute-start.3 = (bf16[192,1536]{1,0:T(8,128)(2,1)S(1)}, bf16[192,1536]{1,0:T(8,128)(2,1)S(1)}, u32[]{:S(2)}, u32[]{:S(2)}) collective-permute-start(bf16[192,1536]{1,0:T(8,128)(2,1)S(1)} %collective-permute-done.2.refs_4_), channel_id=1, source_target_pairs={{0,8},{2,10},{4,12},{6,14},{8,16},{10,18},{12,20},{14,22},{16,24},... | collective-permute-start | bytes 1769480 | tf_op jit(solution)/shard_map/ppermute | solution.py:34
  35.3 0.0 collective-permute-done.6.refs_5_
  35.3 4.6 %collective-permute-start.7 = (bf16[192,1536]{1,0:T(8,128)(2,1)S(1)}, bf16[192,1536]{1,0:T(8,128)(2,1)S(1)}, u32[]{:S(2)}, u32[]{:S(2)}) collective-permute-start(bf16[192,1536]{1,0:T(8,128)(2,1)S(1)} %collective-permute-done.6.refs_5_), channel_id=1, source_target_pairs={{0,56},{2,58},{4,60},{6,62},{8,0},{10,2},{12,4},{14,6},{16,8},{18,... | collective-permute-start | bytes 1769480 | tf_op jit(solution)/shard_map/ppermute | solution.py:34
  39.9 9.4 %collective-permute-done.3.refs_3_ = bf16[192,1536]{1,0:T(8,128)(2,1)S(1)} collective-permute-done((bf16[192,1536]{1,0:T(8,128)(2,1)S(1)}, bf16[192,1536]{1,0:T(8,128)(2,1)S(1)}, u32[]{:S(2)}, u32[]{:S(2)}) %collective-permute-start.3) | collective-permute-done | bytes 589856 | tf_op jit(solution)/shard_map/ppermute | solution.py:34
  49.3 1.9 %collective-permute-start.4 = (bf16[192,1536]{1,0:T(8,128)(2,1)S(1)}, bf16[192,1536]{1,0:T(8,128)(2,1)S(1)}, u32[]{:S(2)}, u32[]{:S(2)}) collective-permute-start(bf16[192,1536]{1,0:T(8,128)(2,1)S(1)} %collective-permute-done.3.refs_3_), channel_id=1, source_target_pairs={{0,8},{2,10},{4,12},{6,14},{8,16},{10,18},{12,20},{14,22},{16,24},... | collective-permute-start | bytes 1769480 | tf_op jit(solution)/shard_map/ppermute | solution.py:34
  51.2 0.0 collective-permute-done.7.refs_4_
  51.2 4.6 %collective-permute-start.8 = (bf16[192,1536]{1,0:T(8,128)(2,1)S(1)}, bf16[192,1536]{1,0:T(8,128)(2,1)S(1)}, u32[]{:S(2)}, u32[]{:S(2)}) collective-permute-start(bf16[192,1536]{1,0:T(8,128)(2,1)S(1)} %collective-permute-done.7.refs_4_), channel_id=1, source_target_pairs={{0,56},{2,58},{4,60},{6,62},{8,0},{10,2},{12,4},{14,6},{16,8},{18,... | collective-permute-start | bytes 1769480 | tf_op jit(solution)/shard_map/ppermute | solution.py:34
  55.8 0.0 copy-done.2
  55.8 3.1 %collective-permute-start.11 = (f32[1,1,256]{2,1,0:T(1,128)S(1)}, f32[1,1,256]{2,1,0:T(1,128)S(1)}, u32[]{:S(2)}, u32[]{:S(2)}) collective-permute-start(f32[1,1,256]{2,1,0:T(1,128)S(1)} %bitcast.1), channel_id=1, source_target_pairs={{0,256},{64,320},{128,384},{192,448},{256,512},{320,576},{384,640}... | collective-permute-start | bytes 3080 | tf_op jit(solution)/shard_map/ppermute | solution.py:239
  58.9 2.2 %collective-permute-start.12 = (f32[1,1,256]{2,1,0:T(1,128)S(1)}, f32[1,1,256]{2,1,0:T(1,128)S(1)}, u32[]{:S(2)}, u32[]{:S(2)}) collective-permute-start(f32[1,1,256]{2,1,0:T(1,128)S(1)} %bitcast.2), channel_id=1, source_target_pairs={{0,512},{64,576},{128,640},{192,704},{256,0},{320,64},{384,128},{4... | collective-permute-start | bytes 3080 | tf_op jit(solution)/shard_map/ppermute | solution.py:239
  61.1 3.2 %collective-permute-done.4.refs_3_ = bf16[192,1536]{1,0:T(8,128)(2,1)S(1)} collective-permute-done((bf16[192,1536]{1,0:T(8,128)(2,1)S(1)}, bf16[192,1536]{1,0:T(8,128)(2,1)S(1)}, u32[]{:S(2)}, u32[]{:S(2)}) %collective-permute-start.4) | collective-permute-done | bytes 589856 | tf_op jit(solution)/shard_map/ppermute | solution.py:34
  64.3 6.6 %collective-permute-start = (bf16[1,176,768]{2,1,0:T(8,128)(2,1)S(1)}, bf16[1,176,768]{2,1,0:T(8,128)(2,1)S(1)}, u32[]{:S(2)}, u32[]{:S(2)}) collective-permute-start(bf16[1,176,768]{2,1,0:T(8,128)(2,1)S(1)} %copy-done), channel_id=1, source_target_pairs={{0,4},{2,6},{4,0},{6,2},{8,12},{10,14},{12,8},{14,10},{16,20},{18,... | collective-permute-start | bytes 811016 | tf_op jit(solution)/shard_map/ppermute | solution.py:34
  70.9 0.0 collective-permute-done.11
  70.9 1.9 %collective-permute-start.5 = (bf16[144,1536]{1,0:T(8,128)(2,1)S(1)}, bf16[144,1536]{1,0:T(8,128)(2,1)S(1)}, u32[]{:S(2)}, u32[]{:S(2)}) collective-permute-start(bf16[144,1536]{1,0:T(8,128)(2,1)S(1)} %slice.8), channel_id=1, source_target_pairs={{0,8},{2,10},{4,12},{6,14},{8,16},{10,18},{12,20},{14,22},{16,24},... | collective-permute-start | bytes 1327112 | tf_op jit(solution)/shard_map/ppermute | solution.py:34
  72.9 0.0 collective-permute-done.12
  72.9 3.1 %collective-permute-start.13 = (f32[3,1,256]{2,1,0:T(1,128)S(1)}, f32[3,1,256]{2,1,0:T(1,128)S(1)}, u32[]{:S(2)}, u32[]{:S(2)}) collective-permute-start(f32[3,1,256]{2,1,0:T(1,128)S(1)} %pad_maximum_fusion.1), channel_id=1, source_target_pairs={{0,64},{64,128},{128,192},{192,0},{256,320},{320,384},{384,448},{4... | collective-permute-start | bytes 9224 | tf_op jit(solution)/shard_map/ppermute | solution.py:239
  76.1 0.0 collective-permute-done.8.refs_4_
  76.1 4.6 %collective-permute-start.9 = (bf16[48,1536]{1,0:T(8,128)(2,1)S(1)}, bf16[48,1536]{1,0:T(8,128)(2,1)S(1)}, u32[]{:S(2)}, u32[]{:S(2)}) collective-permute-start(bf16[48,1536]{1,0:T(8,128)(2,1)S(1)} %slice.9), channel_id=1, source_target_pairs={{0,56},{2,58},{4,60},{6,62},{8,0},{10,2},{12,4},{14,6},{16,8},{18,... | collective-permute-start | bytes 442376 | tf_op jit(solution)/shard_map/ppermute | solution.py:34
  80.7 11.1 %collective-permute-done.refs_2_ = bf16[1,176,768]{2,1,0:T(8,128)(2,1)S(1)} collective-permute-done((bf16[1,176,768]{2,1,0:T(8,128)(2,1)S(1)}, bf16[1,176,768]{2,1,0:T(8,128)(2,1)S(1)}, u32[]{:S(2)}, u32[]{:S(2)}) %collective-permute-start) | collective-permute-done | bytes 270368 | tf_op jit(solution)/shard_map/ppermute | solution.py:34
  91.8 3.8 %shard_map.84 = (f32[768,384]{1,0:T(8,128)S(1)}, f32[16,384]{1,0:T(8,128)S(1)}) custom-call(s32[1,2]{1,0:T(1,128)S(1)} %copy-done.1, bf16[1,176,768]{2,1,0:T(8,128)(2,1)S(1)} %copy-done, bf16[1,176,768]{2,1,0:T(8,128)(2,1)S(1)} %collective-permute-done.refs_2_, bf16[192,1536]{1,0:T(8,128)(2,1)S(1)} %shard_map.83.refs_3_, ...), custom_call_target="tpu_custom_call" | custom-call | flops 679477248 | bytes 2310148 | tf_op jit(solution)/shard_map/pallas_call | solution.py:192
  95.6 3.1 %shard_map.85 = (f32[768,384]{1,0:T(8,128)S(1)}, f32[16,384]{1,0:T(8,128)S(1)}) custom-call(s32[1,2]{1,0:T(1,128)S(1)} %copy-done.1, bf16[1,176,768]{2,1,0:T(8,128)(2,1)S(1)} %copy-done, bf16[1,176,768]{2,1,0:T(8,128)(2,1)S(1)} %collective-permute-done.refs_2_, bf16[192,1536]{1,0:T(8,128)(2,1)S(1)} %collective-permute-done.3.refs_3_, ...), custom_call_target="tpu_custom_call" | custom-call | flops 452984832 | bytes 2322436 | tf_op jit(solution)/shard_map/pallas_call | solution.py:192
  98.7 3.1 %shard_map.86 = (f32[768,384]{1,0:T(8,128)S(1)}, f32[16,384]{1,0:T(8,128)S(1)}) custom-call(s32[1,2]{1,0:T(1,128)S(1)} %copy-done.1, bf16[1,176,768]{2,1,0:T(8,128)(2,1)S(1)} %copy-done, bf16[1,176,768]{2,1,0:T(8,128)(2,1)S(1)} %collective-permute-done.refs_2_, bf16[192,1536]{1,0:T(8,128)(2,1)S(1)} %collective-permute-done.4.refs_3_, ...), custom_call_target="tpu_custom_call" | custom-call | flops 452984832 | bytes 2322436 | tf_op jit(solution)/shard_map/pallas_call | solution.py:192
  101.7 0.0 collective-permute-done.9.refs_4_
  101.8 0.0 collective-permute-done.5.refs_3_
  101.8 2.5 %shard_map.87 = (bf16[184,768]{1,0:T(8,128)(2,1)S(1)}, f32[176,768]{1,0:T(8,128)S(1)}, f32[8,384]{1,0:T(8,128)S(1)}) custom-call(s32[1,2]{1,0:T(1,128)S(1)} %copy-done.1, bf16[1,176,768]{2,1,0:T(8,128)(2,1)S(1)} %copy-done, bf16[1,176,768]{2,1,0:T(8,128)(2,1)S(1)} %collective-permute-done.refs_2_, bf16[144,1536]{1,0:T(8,128)(2,1)S(1)} %collective-permute-done.5.refs_3_, ...), custom_call_target="tpu_custom_call" | custom-call | flops 226492416 | bytes 1732612 | tf_op jit(solution)/shard_map/pallas_call | solution.py:192
  104.3 5.8 %collective-permute-start.10 = (bf16[184,768]{1,0:T(8,128)(2,1)S(1)}, bf16[184,768]{1,0:T(8,128)(2,1)S(1)}, u32[]{:S(2)}, u32[]{:S(2)}) collective-permute-start(bf16[184,768]{1,0:T(8,128)(2,1)S(1)} %get-tuple-element.22), channel_id=1, source_target_pairs={{0,4},{2,6},{4,0},{6,2},{8,12},{10,14},{12,8},{14,10},{16,20},{18,... | collective-permute-start | bytes 847880 | tf_op jit(solution)/shard_map/ppermute | solution.py:34
  110.1 0.0 collective-permute-done.13
  110.1 4.7 %collective-permute-start.14 = (f32[6,1,256]{2,1,0:T(1,128)S(1)}, f32[6,1,256]{2,1,0:T(1,128)S(1)}, u32[]{:S(2)}, u32[]{:S(2)}) collective-permute-start(f32[6,1,256]{2,1,0:T(1,128)S(1)} %pad_maximum_fusion), channel_id=1, source_target_pairs={{0,128},{64,192},{128,0},{192,64},{256,384},{320,448},{384,256},{4... | collective-permute-start | bytes 18440 | tf_op jit(solution)/shard_map/ppermute | solution.py:239
  114.8 1.5 %collective-permute-done.14 = f32[6,1,256]{2,1,0:T(1,128)S(1)} collective-permute-done((f32[6,1,256]{2,1,0:T(1,128)S(1)}, f32[6,1,256]{2,1,0:T(1,128)S(1)}, u32[]{:S(2)}, u32[]{:S(2)}) %collective-permute-start.14) | collective-permute-done | bytes 6176 | tf_op jit(solution)/shard_map/ppermute | solution.py:239
  116.3 9.1 %collective-permute-done.10.got = bf16[184,768]{1,0:T(8,128)(2,1)S(1)} collective-permute-done((bf16[184,768]{1,0:T(8,128)(2,1)S(1)}, bf16[184,768]{1,0:T(8,128)(2,1)S(1)}, u32[]{:S(2)}, u32[]{:S(2)}) %collective-permute-start.10) | collective-permute-done | bytes 282656 | tf_op jit(solution)/shard_map/ppermute | solution.py:34
  125.4 0.5 shard_map.88
  125.8 2.4 %collective-permute-start.15 = (bf16[176,768]{1,0:T(8,128)(2,1)S(1)}, bf16[176,768]{1,0:T(8,128)(2,1)S(1)}, u32[]{:S(2)}, u32[]{:S(2)}) collective-permute-start(bf16[176,768]{1,0:T(8,128)(2,1)S(1)} %get-tuple-element.25.mine), channel_id=1, source_target_pairs={{0,1},{1,0},{2,3},{3,2},{4,5},{5,4},{6,7},{7,6},{8,9},{9,8},{10,11... | collective-permute-start | bytes 811016 | tf_op jit(solution)/shard_map/ppermute | solution.py:38
  128.2 0.6 shard_map.89.partial
  128.8 0.0 collective-permute-done.16.w_got
  128.8 0.5 collective-permute-done.15.theirs
  129.4 1.4 %shard_map.90 = bf16[1,176,1536]{2,1,0:T(8,128)(2,1)} custom-call(f32[176,1536]{1,0:T(8,128)S(1)} %shard_map.89.partial, bf16[176,768]{1,0:T(8,128)(2,1)S(1)} %collective-permute-done.15.theirs, bf16[768,1536]{1,0:T(8,128)(2,1)S(1)} %collective-permute-done.16.w_got, f32[1,1536]{1,0:T(1,128)S(1)} %get-tuple-element.26.gate), custom_call_target="tpu_custom_call" | custom-call | flops 415236096 | bytes 2359296 | tf_op jit(solution)/shard_map/pallas_call | solution.py:315
  (11 shorter events, 0.1 us)
Async XLA Ops:
  0.7 14.3 %collective-permute-start.1 = (bf16[8,1536]{1,0:T(8,128)(2,1)S(1)}, bf16[8,1536]{1,0:T(8,128)(2,1)S(1)}, u32[]{:S(2)}, u32[]{:S(2)}) collective-permute-start(bf16[8,1536]{1,0:T(8,128)(2,1)S(1)} %shard_map.82), channel_id=1, source_target_pairs={{0,6},{2,0},{4,2},{6,4},{8,14},{10,8},{12,10},{14,12},{16,22},{18,... | collective-permute-start | bytes 73736 | tf_op jit(solution)/shard_map/ppermute | solution.py:34
  16.1 17.3 %collective-permute-start.2 = (bf16[192,1536]{1,0:T(8,128)(2,1)S(1)}, bf16[192,1536]{1,0:T(8,128)(2,1)S(1)}, u32[]{:S(2)}, u32[]{:S(2)}) collective-permute-start(bf16[192,1536]{1,0:T(8,128)(2,1)S(1)} %shard_map.83.refs_3_), channel_id=1, source_target_pairs={{0,8},{2,10},{4,12},{6,14},{8,16},{10,18},{12,20},{14,22},{16,24},... | collective-permute-start | bytes 1769480 | tf_op jit(solution)/shard_map/ppermute | solution.py:34
  19.4 36.4 %copy-start.2 = (f32[256]{0:T(256)S(1)}, f32[256]{0:T(256)}, u32[]{:S(2)}) copy-start(f32[256]{0:T(256)} %param.15) | copy-start | bytes 3076
  19.4 44.9 %copy-start = (bf16[1,176,768]{2,1,0:T(8,128)(2,1)S(1)}, bf16[1,176,768]{2,1,0:T(8,128)(2,1)}, u32[]{:S(2)}) copy-start(bf16[1,176,768]{2,1,0:T(8,128)(2,1)} %refs_1_.7) | copy-start | bytes 811012
  19.4 72.4 %copy-start.1 = (s32[1,2]{1,0:T(1,128)S(1)}, s32[1,2]{1,0:T(1,128)}, u32[]{:S(2)}) copy-start(s32[1,2]{1,0:T(1,128)} %refs_0_.7) | copy-start | bytes 28
  19.4 15.9 %collective-permute-start.6 = (bf16[192,1536]{1,0:T(8,128)(2,1)S(1)}, bf16[192,1536]{1,0:T(8,128)(2,1)S(1)}, u32[]{:S(2)}, u32[]{:S(2)}) collective-permute-start(bf16[192,1536]{1,0:T(8,128)(2,1)S(1)} %shard_map.83.refs_3_), channel_id=1, source_target_pairs={{0,56},{2,58},{4,60},{6,62},{8,0},{10,2},{12,4},{14,6},{16,8},{18,... | collective-permute-start | bytes 1769480 | tf_op jit(solution)/shard_map/ppermute | solution.py:34
  26.0 102.8 %collective-permute-start.16 = (bf16[768,1536]{1,0:T(8,128)(2,1)S(1)}, bf16[768,1536]{1,0:T(8,128)(2,1)S(1)}, u32[]{:S(2)}, u32[]{:S(2)}) collective-permute-start(bf16[768,1536]{1,0:T(8,128)(2,1)S(1)} %get-tuple-element.27), channel_id=1, source_target_pairs={{0,1},{1,0},{2,3},{3,2},{4,5},{5,4},{6,7},{7,6},{8,9},{9,8},{10,11... | collective-permute-start | bytes 7077896 | tf_op jit(solution)/shard_map/ppermute | solution.py:38
  33.4 15.9 %collective-permute-start.3 = (bf16[192,1536]{1,0:T(8,128)(2,1)S(1)}, bf16[192,1536]{1,0:T(8,128)(2,1)S(1)}, u32[]{:S(2)}, u32[]{:S(2)}) collective-permute-start(bf16[192,1536]{1,0:T(8,128)(2,1)S(1)} %collective-permute-done.2.refs_4_), channel_id=1, source_target_pairs={{0,8},{2,10},{4,12},{6,14},{8,16},{10,18},{12,20},{14,22},{16,24},... | collective-permute-start | bytes 1769480 | tf_op jit(solution)/shard_map/ppermute | solution.py:34
  35.3 15.9 %collective-permute-start.7 = (bf16[192,1536]{1,0:T(8,128)(2,1)S(1)}, bf16[192,1536]{1,0:T(8,128)(2,1)S(1)}, u32[]{:S(2)}, u32[]{:S(2)}) collective-permute-start(bf16[192,1536]{1,0:T(8,128)(2,1)S(1)} %collective-permute-done.6.refs_5_), channel_id=1, source_target_pairs={{0,56},{2,58},{4,60},{6,62},{8,0},{10,2},{12,4},{14,6},{16,8},{18,... | collective-permute-start | bytes 1769480 | tf_op jit(solution)/shard_map/ppermute | solution.py:34
  49.3 15.0 %collective-permute-start.4 = (bf16[192,1536]{1,0:T(8,128)(2,1)S(1)}, bf16[192,1536]{1,0:T(8,128)(2,1)S(1)}, u32[]{:S(2)}, u32[]{:S(2)}) collective-permute-start(bf16[192,1536]{1,0:T(8,128)(2,1)S(1)} %collective-permute-done.3.refs_3_), channel_id=1, source_target_pairs={{0,8},{2,10},{4,12},{6,14},{8,16},{10,18},{12,20},{14,22},{16,24},... | collective-permute-start | bytes 1769480 | tf_op jit(solution)/shard_map/ppermute | solution.py:34
  51.2 24.8 %collective-permute-start.8 = (bf16[192,1536]{1,0:T(8,128)(2,1)S(1)}, bf16[192,1536]{1,0:T(8,128)(2,1)S(1)}, u32[]{:S(2)}, u32[]{:S(2)}) collective-permute-start(bf16[192,1536]{1,0:T(8,128)(2,1)S(1)} %collective-permute-done.7.refs_4_), channel_id=1, source_target_pairs={{0,56},{2,58},{4,60},{6,62},{8,0},{10,2},{12,4},{14,6},{16,8},{18,... | collective-permute-start | bytes 1769480 | tf_op jit(solution)/shard_map/ppermute | solution.py:34
  55.8 15.1 %collective-permute-start.11 = (f32[1,1,256]{2,1,0:T(1,128)S(1)}, f32[1,1,256]{2,1,0:T(1,128)S(1)}, u32[]{:S(2)}, u32[]{:S(2)}) collective-permute-start(f32[1,1,256]{2,1,0:T(1,128)S(1)} %bitcast.1), channel_id=1, source_target_pairs={{0,256},{64,320},{128,384},{192,448},{256,512},{320,576},{384,640}... | collective-permute-start | bytes 3080 | tf_op jit(solution)/shard_map/ppermute | solution.py:239
  58.9 14.0 %collective-permute-start.12 = (f32[1,1,256]{2,1,0:T(1,128)S(1)}, f32[1,1,256]{2,1,0:T(1,128)S(1)}, u32[]{:S(2)}, u32[]{:S(2)}) collective-permute-start(f32[1,1,256]{2,1,0:T(1,128)S(1)} %bitcast.2), channel_id=1, source_target_pairs={{0,512},{64,576},{128,640},{192,704},{256,0},{320,64},{384,128},{4... | collective-permute-start | bytes 3080 | tf_op jit(solution)/shard_map/ppermute | solution.py:239
  64.3 27.5 %collective-permute-start = (bf16[1,176,768]{2,1,0:T(8,128)(2,1)S(1)}, bf16[1,176,768]{2,1,0:T(8,128)(2,1)S(1)}, u32[]{:S(2)}, u32[]{:S(2)}) collective-permute-start(bf16[1,176,768]{2,1,0:T(8,128)(2,1)S(1)} %copy-done), channel_id=1, source_target_pairs={{0,4},{2,6},{4,0},{6,2},{8,12},{10,14},{12,8},{14,10},{16,20},{18,... | collective-permute-start | bytes 811016 | tf_op jit(solution)/shard_map/ppermute | solution.py:34
  70.9 30.8 %collective-permute-start.5 = (bf16[144,1536]{1,0:T(8,128)(2,1)S(1)}, bf16[144,1536]{1,0:T(8,128)(2,1)S(1)}, u32[]{:S(2)}, u32[]{:S(2)}) collective-permute-start(bf16[144,1536]{1,0:T(8,128)(2,1)S(1)} %slice.8), channel_id=1, source_target_pairs={{0,8},{2,10},{4,12},{6,14},{8,16},{10,18},{12,20},{14,22},{16,24},... | collective-permute-start | bytes 1327112 | tf_op jit(solution)/shard_map/ppermute | solution.py:34
  72.9 37.2 %collective-permute-start.13 = (f32[3,1,256]{2,1,0:T(1,128)S(1)}, f32[3,1,256]{2,1,0:T(1,128)S(1)}, u32[]{:S(2)}, u32[]{:S(2)}) collective-permute-start(f32[3,1,256]{2,1,0:T(1,128)S(1)} %pad_maximum_fusion.1), channel_id=1, source_target_pairs={{0,64},{64,128},{128,192},{192,0},{256,320},{320,384},{384,448},{4... | collective-permute-start | bytes 9224 | tf_op jit(solution)/shard_map/ppermute | solution.py:239
  76.1 25.7 %collective-permute-start.9 = (bf16[48,1536]{1,0:T(8,128)(2,1)S(1)}, bf16[48,1536]{1,0:T(8,128)(2,1)S(1)}, u32[]{:S(2)}, u32[]{:S(2)}) collective-permute-start(bf16[48,1536]{1,0:T(8,128)(2,1)S(1)} %slice.9), channel_id=1, source_target_pairs={{0,56},{2,58},{4,60},{6,62},{8,0},{10,2},{12,4},{14,6},{16,8},{18,... | collective-permute-start | bytes 442376 | tf_op jit(solution)/shard_map/ppermute | solution.py:34
  104.3 21.1 %collective-permute-start.10 = (bf16[184,768]{1,0:T(8,128)(2,1)S(1)}, bf16[184,768]{1,0:T(8,128)(2,1)S(1)}, u32[]{:S(2)}, u32[]{:S(2)}) collective-permute-start(bf16[184,768]{1,0:T(8,128)(2,1)S(1)} %get-tuple-element.22), channel_id=1, source_target_pairs={{0,4},{2,6},{4,0},{6,2},{8,12},{10,14},{12,8},{14,10},{16,20},{18,... | collective-permute-start | bytes 847880 | tf_op jit(solution)/shard_map/ppermute | solution.py:34
  110.1 6.2 %collective-permute-start.14 = (f32[6,1,256]{2,1,0:T(1,128)S(1)}, f32[6,1,256]{2,1,0:T(1,128)S(1)}, u32[]{:S(2)}, u32[]{:S(2)}) collective-permute-start(f32[6,1,256]{2,1,0:T(1,128)S(1)} %pad_maximum_fusion), channel_id=1, source_target_pairs={{0,128},{64,192},{128,0},{192,64},{256,384},{320,448},{384,256},{4... | collective-permute-start | bytes 18440 | tf_op jit(solution)/shard_map/ppermute | solution.py:239
  125.8 3.6 %collective-permute-start.15 = (bf16[176,768]{1,0:T(8,128)(2,1)S(1)}, bf16[176,768]{1,0:T(8,128)(2,1)S(1)}, u32[]{:S(2)}, u32[]{:S(2)}) collective-permute-start(bf16[176,768]{1,0:T(8,128)(2,1)S(1)} %get-tuple-element.25.mine), channel_id=1, source_target_pairs={{0,1},{1,0},{2,3},{3,2},{4,5},{5,4},{6,7},{7,6},{8,9},{9,8},{10,11... | collective-permute-start | bytes 811016 | tf_op jit(solution)/shard_map/ppermute | solution.py:38
